TPU v7x, 256 devices: a whole 4x4x8 slice. The times are simulated.
256 devices in a mesh: dp: 16 (over z_hi, y), ctx: 4 (over x), head: 4 (over z_lo, core).
Axes of the slice: x: 4, y: 4, z: 8 (z_hi: 4, z_lo: 2; z = z_hi * 2 + z_lo), core: 2. Of those that a mesh axis runs over, the one named last changes fastest.
Arguments:
- mix_query: bfloat16 [32768, 8192], P(('dp', 'ctx', 'head')), parts along dimension 0, may hold values from -6 to 6
- mix_key: bfloat16 [32768, 8192], P(('dp', 'ctx', 'head')), parts along dimension 0, may hold values from -6 to 6
- mix_value: bfloat16 [32768, 8192], P(('dp', 'ctx', 'head')), parts along dimension 0, may hold values from -6 to 6
- mr_filter: bfloat16 [512, 128], replicated, may hold values from -0.5 to 0.5
- doc_ids: int32 [32768], P('dp'), parts along dimension 0, may hold values from 0 to 3, never falling along the last dimension, each value on 1 to 1536 neighbouring positions
- att_query: bfloat16 [32768, 4096], P(('dp', 'ctx'), 'head'), parts along dimension 0, may hold values from -5 to 5
- att_key: bfloat16 [32768, 4096], P(('dp', 'ctx'), 'head'), parts along dimension 0, may hold values from -5 to 5
- att_value: bfloat16 [32768, 4096], P(('dp', 'ctx'), 'head'), parts along dimension 0, may hold values from -6 to 6
Outputs:
- mixed: bfloat16 [32768, 8192], P(('dp', 'ctx', 'head')), parts along dimension 0
- attended: bfloat16 [32768, 4096], P(('dp', 'ctx'), 'head'), parts along dimension 0
There are 16 independent parts, one for each index of `dp`. A program takes and returns all parts, laid end to end along the dimension named above; an argument that names none is the same for every part. Nothing has to cross between parts.
Inputs may be any that keep to these rules, and one draw needn't show every extreme that they name: `doc_ids`: document numbers never fall along the sequence; every number occurs; each document covers 1 to 1536 tokens and one covers exactly 1536.
All inputs are finite; a program needn't handle non-finite values.
Results may differ from a plain program's by a relative error of at most 0.0049.
Values may be sent and summed in bfloat16 or wider, within the bound.
No kernel may reach another device: no remote copies, remote signals or barrier semaphores. Data moves between devices by JAX's collectives and lax.ppermute only.
A program may use at most 128 MiB of HBM per device.

v0:
```python
import math

import jax
import jax.numpy as jnp
from jax import lax
from jax.sharding import PartitionSpec as P

HEAD_DIM = 128


NEG_FILL = -1e30


def passed_along(x, axis, by):
    peers = lax.axis_size(axis)
    pairs = [(i, i + by) for i in range(peers) if 0 <= i + by < peers]
    return lax.ppermute(x, axis, pairs)


def toeplitz_rows(filters):
    groups = filters.shape[0]
    filt_len = filters.shape[1]
    lag_index = jnp.arange(filt_len, dtype=jnp.int32)[:, None, None]
    out_index = jnp.arange(filt_len, dtype=jnp.int32)[None, :, None]
    src_index = jnp.arange(2 * filt_len, dtype=jnp.int32)[None, None, :]
    table = (out_index + filt_len - src_index == lag_index).astype(filters.dtype)
    table = table.reshape(filt_len, 2 * filt_len * filt_len)
    kernel = jnp.dot(filters, table, preferred_element_type=jnp.float32).astype(filters.dtype)
    return kernel.reshape(groups, filt_len, 2 * filt_len)


def grouped_conv(extended, seg_ext, filters):
    groups = filters.shape[0]
    filt_len = filters.shape[1]
    channels = extended.shape[1]
    group_size = channels // groups
    blocks = extended.shape[0] // filt_len - 1
    tiled_rows = extended.reshape(blocks + 1, filt_len, groups, group_size)
    paired = jnp.concatenate([tiled_rows[:-1], tiled_rows[1:]], axis=1)
    seg_tiles = seg_ext.reshape(blocks + 1, filt_len)
    seg_pairs = jnp.concatenate([seg_tiles[:-1], seg_tiles[1:]], axis=1)
    same_doc = seg_tiles[1:][:, :, None] == seg_pairs[:, None, :]
    group_step = math.gcd(groups, 64)
    group_blocks = groups // group_step
    pairs_split = jnp.moveaxis(
        paired.reshape(blocks, 2 * filt_len, group_blocks, group_step, group_size), 2, 0
    )
    filt_split = filters.reshape(group_blocks, group_step, filt_len)

    def per_groups(operands):
        part_filters, part_pairs = operands
        kernel = toeplitz_rows(part_filters)
        masked = jnp.where(same_doc[:, None], kernel[None], jnp.zeros((), kernel.dtype))
        return jnp.einsum("bgts,bsgc->btgc", masked, part_pairs, preferred_element_type=jnp.float32)

    results = lax.map(per_groups, (filt_split, pairs_split))
    return jnp.moveaxis(results, 0, 2).reshape(blocks * filt_len, channels)


def initial_state(head_count, row_count):
    return (
        jnp.full((head_count, row_count), NEG_FILL, jnp.float32),
        jnp.zeros((head_count, row_count), jnp.float32),
        jnp.zeros((head_count, row_count, HEAD_DIM), jnp.float32),
    )


def finish(fold_state):
    top_score, denominator, accumulator = fold_state
    scaled = accumulator / denominator[:, :, None]
    row_count = scaled.shape[1]
    return jnp.moveaxis(scaled, 0, 1).reshape(row_count, -1).astype(jnp.bfloat16)


def attend_rows(query_block, key_block, value_block, query_from, key_from, doc_ids, fold_state):
    row_count = query_block.shape[0]
    key_count = key_block.shape[0]
    head_count = query_block.shape[1] // HEAD_DIM
    score_scale = 1.0 / math.sqrt(HEAD_DIM)
    query_docs = lax.dynamic_slice_in_dim(doc_ids, query_from, row_count)
    key_docs = lax.dynamic_slice_in_dim(doc_ids, key_from, key_count)

    def update(state_in):
        top_in, total_in, accum_in = state_in
        scores = (
            jnp.einsum(
                "qhd,khd->hqk",
                query_block.reshape(row_count, head_count, HEAD_DIM),
                key_block.reshape(key_count, head_count, HEAD_DIM),
                preferred_element_type=jnp.float32,
            )
            * score_scale
        )
        query_pos = query_from + jnp.arange(row_count, dtype=jnp.int32)
        key_pos = key_from + jnp.arange(key_count, dtype=jnp.int32)
        allowed = (key_pos[None, :] <= query_pos[:, None]) & (
            key_docs[None, :] == query_docs[:, None]
        )
        masked = jnp.where(allowed[None], scores, NEG_FILL)
        new_top = jnp.maximum(top_in, jnp.max(masked, axis=2))
        weights = jnp.where(allowed[None], jnp.exp(masked - new_top[:, :, None]), 0.0)
        factor = jnp.exp(top_in - new_top)
        total_out = total_in * factor + jnp.sum(weights, axis=2)
        accum_out = accum_in * factor[:, :, None] + jnp.einsum(
            "hqk,khd->hqd",
            weights.astype(jnp.bfloat16),
            value_block.reshape(key_count, head_count, HEAD_DIM),
            preferred_element_type=jnp.float32,
        )
        return (new_top, total_out, accum_out)

    def keep_state(state_in):
        return state_in

    skipped = (key_from > query_from + row_count - 1) | (key_docs[key_count - 1] < query_docs[0])
    return lax.cond(skipped, keep_state, update, fold_state)


def on_device(mix_query, mix_key, mix_value, mr_filter, doc_ids, att_query, att_key, att_value):
    product = (mix_key.astype(jnp.float32) * mix_value.astype(jnp.float32)).astype(jnp.bfloat16)
    filt_len = mr_filter.shape[1]
    tok_rows = mix_query.shape[0]
    device_at = lax.axis_index(("ctx", "head"))
    padded_ids = jnp.concatenate([jnp.full((filt_len,), -1, jnp.int32), doc_ids])
    rim_rows = passed_along(product, ("ctx", "head"), 1)
    extended = jnp.concatenate([rim_rows, product], axis=0)
    local_ids = lax.dynamic_slice_in_dim(padded_ids, device_at * tok_rows, tok_rows + filt_len)
    convolved = grouped_conv(extended, local_ids, mr_filter)
    mixed_out = (mix_query.astype(jnp.float32) * convolved).astype(jnp.bfloat16)
    row_count = att_query.shape[0]
    head_count = att_query.shape[1] // HEAD_DIM
    query_start = lax.axis_index("ctx") * row_count
    key_piece = lax.all_gather(att_key, "ctx", axis=0, tiled=True)
    value_piece = lax.all_gather(att_value, "ctx", axis=0, tiled=True)
    piece_len = key_piece.shape[0]
    block_len = min(piece_len, 512)

    def visit_block(block_at, state_in):
        key_block = lax.dynamic_slice_in_dim(key_piece, block_at * block_len, block_len, 0)
        value_block = lax.dynamic_slice_in_dim(value_piece, block_at * block_len, block_len, 0)
        return attend_rows(
            att_query, key_block, value_block, query_start, block_at * block_len, doc_ids, state_in
        )

    folded = lax.fori_loop(
        0, piece_len // block_len, visit_block, initial_state(head_count, row_count)
    )
    attended = finish(folded)
    return (mixed_out, attended)


def solution(mesh):
    placed = (
        P(("dp", "ctx", "head"), None),
        P(("dp", "ctx", "head"), None),
        P(("dp", "ctx", "head"), None),
        P(),
        P("dp"),
        P(("dp", "ctx"), "head"),
        P(("dp", "ctx"), "head"),
        P(("dp", "ctx"), "head"),
    )
    return jax.shard_map(
        on_device,
        mesh=mesh,
        in_specs=placed,
        out_specs=(P(("dp", "ctx", "head"), None), P(("dp", "ctx"), "head")),
        check_vma=False,
    )
```

profile of v0, /device:TPU:118, one launch (start us, length us, event | category | flops | bytes accessed | tf_op | source)
XLA Modules:
  0.0 191.2 jit_solution(7103810012929130120)
XLA Ops:
  7.2 2.3 %copy.24 = bf16[512,1024]{0,1:T(8,128)(2,1)} copy(bf16[512,1024]{1,0:T(8,128)(2,1)} %param.20) | data formatting | bytes 2097152 | tf_op args[6]
  9.6 2.8 %multiply_convert_fusion = bf16[128,8192]{1,0:T(8,128)(2,1)S(1)} fusion(bf16[128,8192]{1,0:T(8,128)(2,1)} %param.16, bf16[128,8192]{1,0:T(8,128)(2,1)} %param.15), kind=kLoop, calls=%fused_computation.40 | loop fusion | flops 4194304 | bytes 6291456 | tf_op jit(solution)/shard_map/convert_element_type | solution.py:120
  12.4 1.9 %collective-permute-start = (bf16[128,8192]{1,0:T(8,128)(2,1)S(1)}, bf16[128,8192]{1,0:T(8,128)(2,1)}, u32[]{:S(2)}, u32[]{:S(2)}) collective-permute-start(bf16[128,8192]{1,0:T(8,128)(2,1)S(1)} %multiply_convert_fusion), channel_id=1, source_target_pairs={{0,1},{1,2},{2,3},{3,4},{4,5},{5,6},{6,7},{7,8},{8,9},{9,10},{10,1... | collective-permute-start | bytes 6291464 | tf_op jit(solution)/shard_map/ppermute | solution.py:17
  14.3 1.3 copy.25
  15.7 2.4 %copy.22 = bf16[128,8192]{0,1:T(8,128)(2,1)} copy(bf16[128,8192]{1,0:T(8,128)(2,1)S(1)} %multiply_convert_fusion) | data formatting | bytes 4194304 | tf_op jit(solution)/shard_map/convert_element_type | solution.py:120
  18.1 4.1 %copy.20 = bf16[128,8192]{0,1:T(8,128)(2,1)} copy(bf16[128,8192]{1,0:T(8,128)(2,1)} %param.14) | data formatting | bytes 4194304 | tf_op args[0]
  22.4 17.5 %collective-permute-done = bf16[128,8192]{1,0:T(8,128)(2,1)} collective-permute-done((bf16[128,8192]{1,0:T(8,128)(2,1)S(1)}, bf16[128,8192]{1,0:T(8,128)(2,1)}, u32[]{:S(2)}, u32[]{:S(2)}) %collective-permute-start) | collective-permute-done | bytes 2097184 | tf_op jit(solution)/shard_map/ppermute | solution.py:17
  39.8 4.2 %copy.21 = bf16[128,8192]{0,1:T(8,128)(2,1)} copy(bf16[128,8192]{1,0:T(8,128)(2,1)} %collective-permute-done) | data formatting | bytes 4194304 | tf_op jit(solution)/shard_map/ppermute | solution.py:17
  44.1 4.1 %maximum_bitcast_fusion = bf16[8,1,256,64,16]{2,4,3,1,0:T(8,128)(2,1)} fusion(bf16[1,128,8,64,16]{1,4,3,0,2:T(8,128)(2,1)S(1)} %bitcast.102, bf16[1,128,8,64,16]{1,4,3,0,2:T(8,128)(2,1)} %bitcast.103), kind=kLoop, calls=%fused_computation.37 | loop fusion | flops 8388608 | bytes 8388608 | tf_op jit(solution)/shard_map/transpose | solution.py:45
  48.1 78.8 %while.31 = (s32[]{:T(128)}, f32[8,1,128,64,16]{2,4,3,1,0:T(8,128)}, bf16[8,1,256,64,16]{2,4,3,1,0:T(8,128)(2,1)}, bf16[8,64,128]{2,1,0:T(8,128)(2,1)}, s32[256]{0:T(256)S(1)}, /*index=5*/s32[128]{0:T(128)S(1)}, s32[]{:T(128)}) while((s32[]{:T(128)}, f32[8,1,128,64,16]{2,4,3,1,0:T(8,128)}, bf16[8,1,256,64,16]{2,4,3,1,0:T(8,128)(2,1)}, ...), condition=%wide.region_1.2_spmd.clone, body=%wide.region_0.1_spmd.clone.sunk | while | flops 612434048 | bytes 27349068 | solution.py:56
  48.5 4.9 %convolution_convert_fusion.2 = bf16[64,32768]{1,0:T(8,128)(2,1)S(1)} fusion(s32[32768]{0:T(1024)S(1)} %sub.71, bf16[8,64,128]{2,1,0:T(8,128)(2,1)} %get-tuple-element.563, s32[]{:T(128)} %get-tuple-element.553), kind=kOutput, calls=%fused_computation.22.clone.1 | convolution fusion | flops 543162368 | bytes 4342272 | tf_op jit(solution)/shard_map/while/body/eval_jaxpr/dot_general | solution.py:28
  53.3 1.1 copy.45
  55.1 3.1 %fusion.39 = f32[8,1,128,64,16]{2,4,3,1,0:T(8,128)} fusion(f32[8,1,128,64,16]{2,4,3,1,0:T(8,128)} %get-tuple-element.554, s32[]{:T(128)} %get-tuple-element.553, bf16[64,128,256]{2,1,0:T(8,128)(2,1)S(1)} %bitcast_select_fusion.3, bf16[8,1,256,64,16]{2,4,3,1,0:T(8,128)(2,1)} %get-tuple-element.562), kind=kOutput, calls=%fused_computation.27.clone.1 | convolution fusion | flops 67108864 | bytes 5243904 | tf_op jit(solution)/shard_map/while/body/eval_jaxpr/bgts,bsgc->btgc/dot_general | solution.py:54
  58.5 4.7 %convolution_convert_fusion.2 = bf16[64,32768]{1,0:T(8,128)(2,1)S(1)} fusion(s32[32768]{0:T(1024)S(1)} %sub.71, bf16[8,64,128]{2,1,0:T(8,128)(2,1)} %get-tuple-element.563, s32[]{:T(128)} %get-tuple-element.553), kind=kOutput, calls=%fused_computation.22.clone.1 | convolution fusion | flops 543162368 | bytes 4342272 | tf_op jit(solution)/shard_map/while/body/eval_jaxpr/dot_general | solution.py:28
  63.2 1.1 copy.45
  64.4 0.5 bitcast_select_fusion.3
  64.9 3.1 %fusion.39 = f32[8,1,128,64,16]{2,4,3,1,0:T(8,128)} fusion(f32[8,1,128,64,16]{2,4,3,1,0:T(8,128)} %get-tuple-element.554, s32[]{:T(128)} %get-tuple-element.553, bf16[64,128,256]{2,1,0:T(8,128)(2,1)S(1)} %bitcast_select_fusion.3, bf16[8,1,256,64,16]{2,4,3,1,0:T(8,128)(2,1)} %get-tuple-element.562), kind=kOutput, calls=%fused_computation.27.clone.1 | convolution fusion | flops 67108864 | bytes 5243904 | tf_op jit(solution)/shard_map/while/body/eval_jaxpr/bgts,bsgc->btgc/dot_general | solution.py:54
  68.3 4.7 %convolution_convert_fusion.2 = bf16[64,32768]{1,0:T(8,128)(2,1)S(1)} fusion(s32[32768]{0:T(1024)S(1)} %sub.71, bf16[8,64,128]{2,1,0:T(8,128)(2,1)} %get-tuple-element.563, s32[]{:T(128)} %get-tuple-element.553), kind=kOutput, calls=%fused_computation.22.clone.1 | convolution fusion | flops 543162368 | bytes 4342272 | tf_op jit(solution)/shard_map/while/body/eval_jaxpr/dot_general | solution.py:28
  73.0 1.1 copy.45
  74.8 3.1 %fusion.39 = f32[8,1,128,64,16]{2,4,3,1,0:T(8,128)} fusion(f32[8,1,128,64,16]{2,4,3,1,0:T(8,128)} %get-tuple-element.554, s32[]{:T(128)} %get-tuple-element.553, bf16[64,128,256]{2,1,0:T(8,128)(2,1)S(1)} %bitcast_select_fusion.3, bf16[8,1,256,64,16]{2,4,3,1,0:T(8,128)(2,1)} %get-tuple-element.562), kind=kOutput, calls=%fused_computation.27.clone.1 | convolution fusion | flops 67108864 | bytes 5243904 | tf_op jit(solution)/shard_map/while/body/eval_jaxpr/bgts,bsgc->btgc/dot_general | solution.py:54
  78.2 4.7 %convolution_convert_fusion.2 = bf16[64,32768]{1,0:T(8,128)(2,1)S(1)} fusion(s32[32768]{0:T(1024)S(1)} %sub.71, bf16[8,64,128]{2,1,0:T(8,128)(2,1)} %get-tuple-element.563, s32[]{:T(128)} %get-tuple-element.553), kind=kOutput, calls=%fused_computation.22.clone.1 | convolution fusion | flops 543162368 | bytes 4342272 | tf_op jit(solution)/shard_map/while/body/eval_jaxpr/dot_general | solution.py:28
  82.8 1.1 copy.45
  84.0 0.5 bitcast_select_fusion.3
  84.6 3.0 %fusion.39 = f32[8,1,128,64,16]{2,4,3,1,0:T(8,128)} fusion(f32[8,1,128,64,16]{2,4,3,1,0:T(8,128)} %get-tuple-element.554, s32[]{:T(128)} %get-tuple-element.553, bf16[64,128,256]{2,1,0:T(8,128)(2,1)S(1)} %bitcast_select_fusion.3, bf16[8,1,256,64,16]{2,4,3,1,0:T(8,128)(2,1)} %get-tuple-element.562), kind=kOutput, calls=%fused_computation.27.clone.1 | convolution fusion | flops 67108864 | bytes 5243904 | tf_op jit(solution)/shard_map/while/body/eval_jaxpr/bgts,bsgc->btgc/dot_general | solution.py:54
  88.0 4.7 %convolution_convert_fusion.2 = bf16[64,32768]{1,0:T(8,128)(2,1)S(1)} fusion(s32[32768]{0:T(1024)S(1)} %sub.71, bf16[8,64,128]{2,1,0:T(8,128)(2,1)} %get-tuple-element.563, s32[]{:T(128)} %get-tuple-element.553), kind=kOutput, calls=%fused_computation.22.clone.1 | convolution fusion | flops 543162368 | bytes 4342272 | tf_op jit(solution)/shard_map/while/body/eval_jaxpr/dot_general | solution.py:28
  92.6 1.1 copy.45
  94.4 3.1 %fusion.39 = f32[8,1,128,64,16]{2,4,3,1,0:T(8,128)} fusion(f32[8,1,128,64,16]{2,4,3,1,0:T(8,128)} %get-tuple-element.554, s32[]{:T(128)} %get-tuple-element.553, bf16[64,128,256]{2,1,0:T(8,128)(2,1)S(1)} %bitcast_select_fusion.3, bf16[8,1,256,64,16]{2,4,3,1,0:T(8,128)(2,1)} %get-tuple-element.562), kind=kOutput, calls=%fused_computation.27.clone.1 | convolution fusion | flops 67108864 | bytes 5243904 | tf_op jit(solution)/shard_map/while/body/eval_jaxpr/bgts,bsgc->btgc/dot_general | solution.py:54
  97.8 4.7 %convolution_convert_fusion.2 = bf16[64,32768]{1,0:T(8,128)(2,1)S(1)} fusion(s32[32768]{0:T(1024)S(1)} %sub.71, bf16[8,64,128]{2,1,0:T(8,128)(2,1)} %get-tuple-element.563, s32[]{:T(128)} %get-tuple-element.553), kind=kOutput, calls=%fused_computation.22.clone.1 | convolution fusion | flops 543162368 | bytes 4342272 | tf_op jit(solution)/shard_map/while/body/eval_jaxpr/dot_general | solution.py:28
  102.4 1.1 copy.45
  104.2 3.1 %fusion.39 = f32[8,1,128,64,16]{2,4,3,1,0:T(8,128)} fusion(f32[8,1,128,64,16]{2,4,3,1,0:T(8,128)} %get-tuple-element.554, s32[]{:T(128)} %get-tuple-element.553, bf16[64,128,256]{2,1,0:T(8,128)(2,1)S(1)} %bitcast_select_fusion.3, bf16[8,1,256,64,16]{2,4,3,1,0:T(8,128)(2,1)} %get-tuple-element.562), kind=kOutput, calls=%fused_computation.27.clone.1 | convolution fusion | flops 67108864 | bytes 5243904 | tf_op jit(solution)/shard_map/while/body/eval_jaxpr/bgts,bsgc->btgc/dot_general | solution.py:54
  107.6 4.7 %convolution_convert_fusion.2 = bf16[64,32768]{1,0:T(8,128)(2,1)S(1)} fusion(s32[32768]{0:T(1024)S(1)} %sub.71, bf16[8,64,128]{2,1,0:T(8,128)(2,1)} %get-tuple-element.563, s32[]{:T(128)} %get-tuple-element.553), kind=kOutput, calls=%fused_computation.22.clone.1 | convolution fusion | flops 543162368 | bytes 4342272 | tf_op jit(solution)/shard_map/while/body/eval_jaxpr/dot_general | solution.py:28
  112.3 1.1 copy.45
  114.0 3.1 %fusion.39 = f32[8,1,128,64,16]{2,4,3,1,0:T(8,128)} fusion(f32[8,1,128,64,16]{2,4,3,1,0:T(8,128)} %get-tuple-element.554, s32[]{:T(128)} %get-tuple-element.553, bf16[64,128,256]{2,1,0:T(8,128)(2,1)S(1)} %bitcast_select_fusion.3, bf16[8,1,256,64,16]{2,4,3,1,0:T(8,128)(2,1)} %get-tuple-element.562), kind=kOutput, calls=%fused_computation.27.clone.1 | convolution fusion | flops 67108864 | bytes 5243904 | tf_op jit(solution)/shard_map/while/body/eval_jaxpr/bgts,bsgc->btgc/dot_general | solution.py:54
  117.4 4.7 %convolution_convert_fusion.2 = bf16[64,32768]{1,0:T(8,128)(2,1)S(1)} fusion(s32[32768]{0:T(1024)S(1)} %sub.71, bf16[8,64,128]{2,1,0:T(8,128)(2,1)} %get-tuple-element.563, s32[]{:T(128)} %get-tuple-element.553), kind=kOutput, calls=%fused_computation.22.clone.1 | convolution fusion | flops 543162368 | bytes 4342272 | tf_op jit(solution)/shard_map/while/body/eval_jaxpr/dot_general | solution.py:28
  122.1 1.1 copy.45
  123.9 3.1 %fusion.39 = f32[8,1,128,64,16]{2,4,3,1,0:T(8,128)} fusion(f32[8,1,128,64,16]{2,4,3,1,0:T(8,128)} %get-tuple-element.554, s32[]{:T(128)} %get-tuple-element.553, bf16[64,128,256]{2,1,0:T(8,128)(2,1)S(1)} %bitcast_select_fusion.3, bf16[8,1,256,64,16]{2,4,3,1,0:T(8,128)(2,1)} %get-tuple-element.562), kind=kOutput, calls=%fused_computation.27.clone.1 | convolution fusion | flops 67108864 | bytes 5243904 | tf_op jit(solution)/shard_map/while/body/eval_jaxpr/bgts,bsgc->btgc/dot_general | solution.py:54
  127.0 4.0 %fusion.24 = bf16[128,8192]{0,1:T(8,128)(2,1)} fusion(f32[8,1,128,64,16]{2,4,3,1,0:T(8,128)} %get-tuple-element.364, bf16[128,8192]{0,1:T(8,128)(2,1)S(1)} %copy-done.1), kind=kLoop, calls=%fused_computation.39 | loop fusion | flops 3145728 | bytes 8388608 | tf_op jit(solution)/shard_map/convert_element_type | solution.py:129
  130.9 4.2 %copy.27 = bf16[128,8192]{1,0:T(8,128)(2,1)} copy(bf16[128,8192]{0,1:T(8,128)(2,1)} %fusion.24) | data formatting | bytes 4194304
  135.2 47.6 %while.30 = (s32[]{:T(128)}, f32[8,512]{1,0:T(8,128)S(1)}, f32[8,512]{1,0:T(8,128)S(1)}, f32[8,512,128]{2,1,0:T(8,128)S(1)}, s32[]{:T(128)}, /*index=5*/s32[2048...) while((s32[]{:T(128)}, f32[8,512]{1,0:T(8,128)S(1)}, ...), condition=%wide.region_7.8_spmd, body=%wide.region_2.7_spmd.sunk | while | flops 1102849024 | bytes 38027644 | solution.py:145
  135.5 0.6 slice.44
  137.8 9.5 %conditional.2 = (f32[8,512]{1,0:T(8,128)S(1)}, f32[8,512]{1,0:T(8,128)S(1)}, f32[8,512,128]{2,1,0:T(8,128)S(1)}) conditional(s32[]{:T(128)} %convert_element_type.67, (s32[]{:T(128)}, s32[]{:T(128)}, s32[512]{0:T(512)S(1)}, s32[512]{0:T(512)S(1)}, bf16[2048,1024]{0,1:T(8,128)(2,1)}, /*index=5*/s32[]{:T(128)}, bf16[512,1024]{1,0:T(8,128)(2,1)S(1)}, ...), branch_computations={%region_3.5_spmd, %region_6.6_spmd} | conditional | flops 1102849024 | bytes 37990436 | solution.py:116
  138.1 1.7 constant_dynamic-slice_fusion
  139.8 1.8 fusion.2
  141.6 2.0 %fusion.4 = f32[8,512]{1,0:T(8,128)S(1)} fusion(f32[8,512,512]{2,1,0:T(8,128)S(1)} %get-tuple-element.422, f32[8,512]{1,0:T(8,128)S(1)} %max.4, pred[512,512]{0,1:T(8,128)(4,1)S(1)} %compare_and_fusion), kind=kLoop, calls=%fused_computation.5 | loop fusion | flops 10481664 | bytes 8683520 | tf_op jit(solution)/shard_map/while/body/eval_jaxpr/cond/branch_0_fun/reduce_sum | solution.py:103
  143.6 3.6 %multiply_add_fusion = f32[8,512,128]{2,1,0:T(8,128)S(1)} fusion(f32[8,512,128]{2,1,0:T(8,128)S(1)} %get-tuple-element.342, bf16[512,8,128]{0,2,1:T(8,128)(2,1)S(1)} %bitcast.99, f32[8,512,512]{2,1,0:T(8,128)S(1)} %get-tuple-element.422, f32[8,512]{1,0:T(8,128)S(1)} %max.4, pred[512,512]{0,1:T(8,128)(4,1)S(1)} %compare_and_fusion, ...), kind=kOutput, calls=%fused_computation.8 | convolution fusion | flops 548405248 | bytes 13926400 | tf_op jit(solution)/shard_map/while/body/eval_jaxpr/cond/branch_0_fun/hqk,khd->hqd/dot_general | solution.py:104
  147.4 0.6 slice.44
  149.6 9.5 %conditional.2 = (f32[8,512]{1,0:T(8,128)S(1)}, f32[8,512]{1,0:T(8,128)S(1)}, f32[8,512,128]{2,1,0:T(8,128)S(1)}) conditional(s32[]{:T(128)} %convert_element_type.67, (s32[]{:T(128)}, s32[]{:T(128)}, s32[512]{0:T(512)S(1)}, s32[512]{0:T(512)S(1)}, bf16[2048,1024]{0,1:T(8,128)(2,1)}, /*index=5*/s32[]{:T(128)}, bf16[512,1024]{1,0:T(8,128)(2,1)S(1)}, ...), branch_computations={%region_3.5_spmd, %region_6.6_spmd} | conditional | flops 1102849024 | bytes 37990436 | solution.py:116
  149.9 1.7 constant_dynamic-slice_fusion
  151.6 1.8 fusion.2
  153.4 2.0 %fusion.4 = f32[8,512]{1,0:T(8,128)S(1)} fusion(f32[8,512,512]{2,1,0:T(8,128)S(1)} %get-tuple-element.422, f32[8,512]{1,0:T(8,128)S(1)} %max.4, pred[512,512]{0,1:T(8,128)(4,1)S(1)} %compare_and_fusion), kind=kLoop, calls=%fused_computation.5 | loop fusion | flops 10481664 | bytes 8683520 | tf_op jit(solution)/shard_map/while/body/eval_jaxpr/cond/branch_0_fun/reduce_sum | solution.py:103
  155.5 3.6 %multiply_add_fusion = f32[8,512,128]{2,1,0:T(8,128)S(1)} fusion(f32[8,512,128]{2,1,0:T(8,128)S(1)} %get-tuple-element.342, bf16[512,8,128]{0,2,1:T(8,128)(2,1)S(1)} %bitcast.99, f32[8,512,512]{2,1,0:T(8,128)S(1)} %get-tuple-element.422, f32[8,512]{1,0:T(8,128)S(1)} %max.4, pred[512,512]{0,1:T(8,128)(4,1)S(1)} %compare_and_fusion, ...), kind=kOutput, calls=%fused_computation.8 | convolution fusion | flops 548405248 | bytes 13926400 | tf_op jit(solution)/shard_map/while/body/eval_jaxpr/cond/branch_0_fun/hqk,khd->hqd/dot_general | solution.py:104
  159.2 0.6 slice.44
  161.5 9.5 %conditional.2 = (f32[8,512]{1,0:T(8,128)S(1)}, f32[8,512]{1,0:T(8,128)S(1)}, f32[8,512,128]{2,1,0:T(8,128)S(1)}) conditional(s32[]{:T(128)} %convert_element_type.67, (s32[]{:T(128)}, s32[]{:T(128)}, s32[512]{0:T(512)S(1)}, s32[512]{0:T(512)S(1)}, bf16[2048,1024]{0,1:T(8,128)(2,1)}, /*index=5*/s32[]{:T(128)}, bf16[512,1024]{1,0:T(8,128)(2,1)S(1)}, ...), branch_computations={%region_3.5_spmd, %region_6.6_spmd} | conditional | flops 1102849024 | bytes 37990436 | solution.py:116
  161.8 1.7 constant_dynamic-slice_fusion
  163.5 1.8 fusion.2
  165.3 2.0 %fusion.4 = f32[8,512]{1,0:T(8,128)S(1)} fusion(f32[8,512,512]{2,1,0:T(8,128)S(1)} %get-tuple-element.422, f32[8,512]{1,0:T(8,128)S(1)} %max.4, pred[512,512]{0,1:T(8,128)(4,1)S(1)} %compare_and_fusion), kind=kLoop, calls=%fused_computation.5 | loop fusion | flops 10481664 | bytes 8683520 | tf_op jit(solution)/shard_map/while/body/eval_jaxpr/cond/branch_0_fun/reduce_sum | solution.py:103
  167.3 3.6 %multiply_add_fusion = f32[8,512,128]{2,1,0:T(8,128)S(1)} fusion(f32[8,512,128]{2,1,0:T(8,128)S(1)} %get-tuple-element.342, bf16[512,8,128]{0,2,1:T(8,128)(2,1)S(1)} %bitcast.99, f32[8,512,512]{2,1,0:T(8,128)S(1)} %get-tuple-element.422, f32[8,512]{1,0:T(8,128)S(1)} %max.4, pred[512,512]{0,1:T(8,128)(4,1)S(1)} %compare_and_fusion, ...), kind=kOutput, calls=%fused_computation.8 | convolution fusion | flops 548405248 | bytes 13926400 | tf_op jit(solution)/shard_map/while/body/eval_jaxpr/cond/branch_0_fun/hqk,khd->hqd/dot_general | solution.py:104
  171.1 0.6 slice.44
  173.4 9.5 %conditional.2 = (f32[8,512]{1,0:T(8,128)S(1)}, f32[8,512]{1,0:T(8,128)S(1)}, f32[8,512,128]{2,1,0:T(8,128)S(1)}) conditional(s32[]{:T(128)} %convert_element_type.67, (s32[]{:T(128)}, s32[]{:T(128)}, s32[512]{0:T(512)S(1)}, s32[512]{0:T(512)S(1)}, bf16[2048,1024]{0,1:T(8,128)(2,1)}, /*index=5*/s32[]{:T(128)}, bf16[512,1024]{1,0:T(8,128)(2,1)S(1)}, ...), branch_computations={%region_3.5_spmd, %region_6.6_spmd} | conditional | flops 1102849024 | bytes 37990436 | solution.py:116
  173.7 1.7 constant_dynamic-slice_fusion
  175.4 1.8 fusion.2
  177.1 2.0 %fusion.4 = f32[8,512]{1,0:T(8,128)S(1)} fusion(f32[8,512,512]{2,1,0:T(8,128)S(1)} %get-tuple-element.422, f32[8,512]{1,0:T(8,128)S(1)} %max.4, pred[512,512]{0,1:T(8,128)(4,1)S(1)} %compare_and_fusion), kind=kLoop, calls=%fused_computation.5 | loop fusion | flops 10481664 | bytes 8683520 | tf_op jit(solution)/shard_map/while/body/eval_jaxpr/cond/branch_0_fun/reduce_sum | solution.py:103
  179.2 3.6 %multiply_add_fusion = f32[8,512,128]{2,1,0:T(8,128)S(1)} fusion(f32[8,512,128]{2,1,0:T(8,128)S(1)} %get-tuple-element.342, bf16[512,8,128]{0,2,1:T(8,128)(2,1)S(1)} %bitcast.99, f32[8,512,512]{2,1,0:T(8,128)S(1)} %get-tuple-element.422, f32[8,512]{1,0:T(8,128)S(1)} %max.4, pred[512,512]{0,1:T(8,128)(4,1)S(1)} %compare_and_fusion, ...), kind=kOutput, calls=%fused_computation.8 | convolution fusion | flops 548405248 | bytes 13926400 | tf_op jit(solution)/shard_map/while/body/eval_jaxpr/cond/branch_0_fun/hqk,khd->hqd/dot_general | solution.py:104
  182.9 1.5 copy_bitcast_fusion
  (106 shorter events, 10.2 us)
Async XLA Ops:
  7.2 127.9 %all-gather.3.cloned.1.call-start = ((), (), s32[]{:S(2)}) async-start(), calls=%async_computation | async-start | bytes 5242880 | tf_op jit(solution)/shard_map/all_gather | solution.py:133
  9.5 4.8 %copy-start.3 = (bf16[512,1024]{1,0:T(8,128)(2,1)S(1)}, bf16[512,1024]{1,0:T(8,128)(2,1)}, u32[]{:S(2)}) copy-start(bf16[512,1024]{1,0:T(8,128)(2,1)} %param.21) | copy-start | bytes 3145732
  9.5 125.6 %all-gather.5.cloned.1.call-start = ((), (), s32[]{:S(2)}) async-start(), calls=%async_computation.1 | async-start | bytes 5242880 | tf_op jit(solution)/shard_map/all_gather | solution.py:134
  12.4 27.5 %collective-permute-start = (bf16[128,8192]{1,0:T(8,128)(2,1)S(1)}, bf16[128,8192]{1,0:T(8,128)(2,1)}, u32[]{:S(2)}, u32[]{:S(2)}) collective-permute-start(bf16[128,8192]{1,0:T(8,128)(2,1)S(1)} %multiply_convert_fusion), channel_id=1, source_target_pairs={{0,1},{1,2},{2,3},{3,4},{4,5},{5,6},{6,7},{7,8},{8,9},{9,10},{10,1... | collective-permute-start | bytes 6291464 | tf_op jit(solution)/shard_map/ppermute | solution.py:17
  15.7 6.5 %copy-start.4 = (s32[2048]{0:T(1024)S(1)}, s32[2048]{0:T(1024)}, u32[]{:S(2)}) copy-start(s32[2048]{0:T(1024)} %param.18) | copy-start | bytes 24580
  39.8 4.2 %copy-start.2 = (bf16[128,8192]{0,1:T(8,128)(2,1)S(1)}, bf16[128,8192]{0,1:T(8,128)(2,1)}, u32[]{:S(2)}) copy-start(bf16[128,8192]{0,1:T(8,128)(2,1)} %copy.22) | copy-start | bytes 6291460
  48.1 78.8 %copy-start.1 = (bf16[128,8192]{0,1:T(8,128)(2,1)S(1)}, bf16[128,8192]{0,1:T(8,128)(2,1)}, u32[]{:S(2)}) copy-start(bf16[128,8192]{0,1:T(8,128)(2,1)} %copy.20) | copy-start | bytes 6291460
  130.9 4.3 %copy-start = (bf16[512,1024]{1,0:T(8,128)(2,1)S(1)}, bf16[512,1024]{1,0:T(8,128)(2,1)}, u32[]{:S(2)}) copy-start(bf16[512,1024]{1,0:T(8,128)(2,1)} %param.19) | copy-start | bytes 3145732
Sparse Core Ops, SparseCore 0:
  10.4 50.8 all-gather.2
  63.1 64.2 all-gather.4
where the time goes:
time: 194 us; the launch traced here: 191 us
  matrix products  83.6 us (43%)
  local copies, waits for them, and re-layouts  41.3 us (21%)
  other arithmetic  26.9 us (14%)
  waiting for transfers between devices  17.5 us (9%)
  between operations  14.1 us (7%)
  loops' own time  5.79 us (3%)
  starting transfers between devices  2 us (1%)
    dot_general x8, matrix products, toeplitz_rows(): jnp.dot(filters, table, preferred_element_type=jnp.float32)  37.5 us
    dot_general x8, matrix products, per_groups(): jnp.einsum('bgts,bsgc->btgc', masked, part_pairs, preferred_element_type=...  24.5 us
    ppermute x1, waiting for transfers between devices, passed_along(): return lax.ppermute(x, axis, pairs)  17.5 us
    dot_general x4, matrix products, update(): jnp.einsum('hqk,khd->hqd', weights.astype(jnp.bfloat16), value_block.resh...  14.5 us
    unnamed x14, local copies, waits for them, and re-layouts  11.9 us
    while x28, local copies, waits for them, and re-layouts  9.53 us
    reduce_sum x4, other arithmetic, update(): total_out = total_in * factor + jnp.sum(weights, axis=2)  8.13 us
    dot_general x4, matrix products, update(): jnp.einsum('qhd,khd->hqk', query_block.reshape(row_count, head_count, HEA...  7.01 us
  transfers between devices with their start and end apart: 3, of which 1 were waited for; matrix products, arithmetic and copies ran while one was open for 55% of the time, Pallas kernels for 0%

commit v1 on v0

v1 whole, which is shorter than its diff:
```python
import functools
import math

import jax
import jax.numpy as jnp
from jax import lax
from jax.experimental import pallas as pl
from jax.experimental.pallas import tpu as pltpu
from jax.sharding import PartitionSpec as P

HEAD_DIM = 128
NEG_FILL = -1e30
LOG2_SCALE = math.log2(math.e) / math.sqrt(HEAD_DIM)
SIDE = 4
SUB = 256
EXTRA = 16
COLS = 1024
HEADS_AXIS = 4


def pick(at, *values):
    out = jnp.int32(values[-1])
    for i in range(len(values) - 2, -1, -1):
        out = jnp.where(at == i, jnp.int32(values[i]), out)
    return out


def first_of(bounds, position):
    first = jnp.zeros_like(position)
    for doc in range(1, 4):
        first = jnp.where(bounds[doc] <= position, bounds[doc], first)
    return first


def conv_kernel(group_size, place, bounds, rim_a_ref, rim_b_ref, prod_ref, query_ref, filt_ref, out_ref, mask):
    rows, cols = prod_ref.shape
    step = pl.program_id(0)

    @pl.when(step == 0)
    def _():
        token = place[0] * rows + lax.broadcasted_iota(jnp.int32, (2 * rows, rows), 1)
        source = (place[0] - 1) * rows + lax.broadcasted_iota(jnp.int32, (2 * rows, rows), 0)
        allowed = (source <= token) & (source > token - rows) & (source >= first_of(bounds, token))
        mask[...] = jnp.where(allowed, 1.0, 0.0).astype(jnp.bfloat16)

    rim = jnp.where(step < pl.num_programs(0) // 2, rim_a_ref[...], rim_b_ref[...])
    turned = jnp.concatenate([rim, prod_ref[...]], axis=0).T
    filters = filt_ref[...].astype(jnp.float32)
    allowed = mask[...]
    parts = []
    for g in range(cols // group_size):
        line = jnp.broadcast_to(filters[g : g + 1, :], (rows, rows))
        ring = pltpu.roll(line, 0, 1, stride=1, stride_axis=0).astype(jnp.bfloat16)
        taps = jnp.concatenate([ring, ring], axis=0) * allowed
        parts.append(
            jnp.dot(turned[g * group_size : (g + 1) * group_size], taps, preferred_element_type=jnp.float32)
        )
    total = jnp.concatenate(parts, axis=0).T
    out_ref[...] = (query_ref[...].astype(jnp.float32) * total).astype(out_ref.dtype)


def mixer(place, bounds, rim_a, rim_b, product, mix_query, mr_filter):
    rows, width = product.shape
    groups, filt_len = mr_filter.shape
    group_size = width // groups
    steps = width // COLS
    tile = pl.BlockSpec((rows, COLS), lambda i, *_: (0, i))
    return pl.pallas_call(
        functools.partial(conv_kernel, group_size),
        out_shape=jax.ShapeDtypeStruct((rows, width), jnp.bfloat16),
        grid_spec=pltpu.PrefetchScalarGridSpec(
            num_scalar_prefetch=2,
            grid=(steps,),
            in_specs=[
                pl.BlockSpec((rows, COLS), lambda i, *_: (0, jnp.minimum(i, steps // 2 - 1))),
                pl.BlockSpec((rows, COLS), lambda i, *_: (0, jnp.maximum(i - steps // 2, 0))),
                tile,
                tile,
                pl.BlockSpec((COLS // group_size, filt_len), lambda i, *_: (i, 0)),
            ],
            out_specs=tile,
            scratch_shapes=[pltpu.VMEM((2 * rows, rows), jnp.bfloat16)],
        ),
        cost_estimate=pl.CostEstimate(
            flops=2 * rows * 2 * filt_len * width * 16, bytes_accessed=8 * rows * width, transcendentals=0
        ),
        name="mixer",
    )(place, bounds, rim_a, rim_b, product, mix_query, mr_filter)


def cols_of(h):
    return slice(h * HEAD_DIM, (h + 1) * HEAD_DIM)


def fold_tiles(bounds, query_block, query, sources, heads, state, finish):
    top, den, acc, turned_q, turned_v = state
    rows = query.shape[0]
    turned_q[...] = query.T
    whole_lowest = first_of(bounds, query_block * rows)
    for n, (block, _, value_of) in enumerate(sources):

        @pl.when((block >= 0) & (block <= query_block) & ((block + 1) * rows > whole_lowest))
        def _(n=n, value_of=value_of):
            turned_v[n] = value_of().T

    for part in range(rows // SUB):
        at = pl.ds(part * SUB, SUB)
        query_from = query_block * rows + part * SUB
        line_pos = query_from + lax.broadcasted_iota(jnp.int32, (1, SUB), 1)
        first_row = first_of(bounds, line_pos)
        lowest = first_of(bounds, query_from)
        top[...] = jnp.full(top.shape, 0.5 * NEG_FILL, jnp.float32)
        den[...] = jnp.zeros(den.shape, jnp.float32)
        acc[...] = jnp.zeros(acc.shape, jnp.float32)
        for n, (block, key_of, _) in enumerate(sources):
            for piece in range(rows // SUB):
                key_from = block * rows + piece * SUB
                needed = (block >= 0) & (key_from <= query_from) & (key_from + SUB > lowest)

                @pl.when(needed)
                def _(n=n, key_of=key_of, piece=piece, key_from=key_from):
                    take = pl.ds(piece * SUB, SUB)
                    key_pos = key_from + lax.broadcasted_iota(jnp.int32, (SUB, SUB), 0)
                    allowed = (key_pos <= line_pos) & (key_pos >= first_row)
                    scores = [
                        jnp.dot(key_of(h, take), turned_q[cols_of(h), at], preferred_element_type=jnp.float32)
                        for h in range(heads)
                    ]
                    ready = []
                    for h in range(heads):
                        masked = jnp.where(allowed, scores[h], NEG_FILL)
                        old = top[h]
                        new = jnp.maximum(old, jnp.max(masked, axis=0, keepdims=True))
                        weights = jnp.exp2((masked - new) * LOG2_SCALE)
                        factor = jnp.exp2((old - new) * LOG2_SCALE)
                        den[h] = den[h] * factor + jnp.sum(weights, axis=0, keepdims=True)
                        top[h] = new
                        ready.append((weights.astype(jnp.bfloat16), factor))
                    for h, (weights, factor) in enumerate(ready):
                        acc[h] = acc[h] * factor + jnp.dot(
                            turned_v[n, cols_of(h), take], weights, preferred_element_type=jnp.float32
                        )

        for h in range(heads):
            some = den[h] > 0.0
            safe = jnp.where(some, den[h], 1.0)
            lse = jnp.where(some, top[h] * LOG2_SCALE + jnp.log2(safe), NEG_FILL)
            finish(h, at, acc[h] / safe, lse)


def send_kernel(side, place, bounds, qa_ref, qb_ref, k_ref, v_ref, kv_ref, out_ref, *state):
    ctx = place[0] // HEADS_AXIS
    if side == 0:
        query_block, got_block = pick(ctx, 3, 2, 3, 0), pick(ctx, 1, 0, -1, -1)
        second, active = ctx == 2, ctx != 3
    else:
        query_block, got_block = pick(ctx, 1, 0, 3, 2), pick(ctx, -1, -1, 1, 0)
        second, active = ctx == 0, ctx != 1

    def finish(h, at, scaled, lse):
        out_ref[h, :HEAD_DIM, at] = scaled.astype(jnp.bfloat16)
        high = lse.astype(jnp.bfloat16).astype(jnp.float32)
        mid = (lse - high).astype(jnp.bfloat16).astype(jnp.float32)
        low = lse - high - mid
        line = lax.broadcasted_iota(jnp.int32, (EXTRA, SUB), 0)
        lines = jnp.where(line == 0, high, jnp.where(line == 1, mid, low))
        out_ref[h, HEAD_DIM:, at] = lines.astype(jnp.bfloat16)

    @pl.when(active)
    def _():
        query = jnp.where(second, qb_ref[...], qa_ref[...])
        sources = [
            (ctx, lambda h, take: k_ref[take, cols_of(h)], lambda: v_ref[...]),
            (got_block, lambda h, take: kv_ref[0, take, cols_of(h)], lambda: kv_ref[1]),
        ]
        fold_tiles(bounds, query_block, query, sources, SIDE, state, finish)


def keep_kernel(mode, place, bounds, q_ref, *rest):
    ctx = place[0] // HEADS_AXIS
    if mode is None:
        k_ref, v_ref, out_ref, lse_ref, *state = rest
        block, active = ctx, ctx >= 0
        source = (block, lambda h, take: k_ref[take, cols_of(h)], lambda: v_ref[...])
    else:
        kv_ref, out_ref, lse_ref, *state = rest
        block = pick(ctx, -1, 0, -1, -1) if mode == 0 else pick(ctx, -1, -1, 1, 0)
        active = block >= 0
        source = (block, lambda h, take: kv_ref[0, take, cols_of(h)], lambda: kv_ref[1])

    def finish(h, at, scaled, lse):
        out_ref[h, :, at] = scaled
        lse_ref[h, :, at] = jnp.broadcast_to(lse, (8, SUB))

    @pl.when(active)
    def _():
        fold_tiles(bounds, ctx, q_ref[...], [source], SIDE, state, finish)


def state_shapes(rows, sources):
    return [
        pltpu.VMEM((SIDE, 1, SUB), jnp.float32),
        pltpu.VMEM((SIDE, 1, SUB), jnp.float32),
        pltpu.VMEM((SIDE, HEAD_DIM, SUB), jnp.float32),
        pltpu.VMEM((SIDE * HEAD_DIM, rows), jnp.bfloat16),
        pltpu.VMEM((sources, SIDE * HEAD_DIM, rows), jnp.bfloat16),
    ]


def cost(rows, blocks, heads):
    return pl.CostEstimate(flops=1, bytes_accessed=1, transcendentals=0)


def fold_send(side, place, bounds, qa, qb, keys, values, got_kv):
    rows = keys.shape[0]
    half = SIDE * HEAD_DIM
    whole = pl.BlockSpec((rows, half), lambda i, *_: (0, 0))
    mine = pl.BlockSpec((rows, half), lambda i, *_: (0, side))
    return pl.pallas_call(
        functools.partial(send_kernel, side),
        out_shape=jax.ShapeDtypeStruct((SIDE, HEAD_DIM + EXTRA, rows), jnp.bfloat16),
        grid_spec=pltpu.PrefetchScalarGridSpec(
            num_scalar_prefetch=2,
            grid=(1,),
            in_specs=[whole, whole, mine, mine, pl.BlockSpec((2, rows, half), lambda i, *_: (0, 0, 0))],
            out_specs=pl.BlockSpec((SIDE, HEAD_DIM + EXTRA, rows), lambda i, *_: (0, 0, 0)),
            scratch_shapes=state_shapes(rows, 2),
        ),
        cost_estimate=cost(rows, 2, SIDE),
        name="fold_send",
    )(place, bounds, qa, qb, keys, values, got_kv)


def fold_keep(mode, place, bounds, queries, *pairs):
    rows, width = queries.shape
    half = SIDE * HEAD_DIM
    if mode is None:
        steps, spec = width // half, pl.BlockSpec((rows, half), lambda i, *_: (0, i))
        in_specs = [spec, spec, spec]
    else:
        steps = 1
        in_specs = [
            pl.BlockSpec((rows, half), lambda i, *_: (0, mode)),
            pl.BlockSpec((2, rows, half), lambda i, *_: (0, 0, 0)),
        ]
    return pl.pallas_call(
        functools.partial(keep_kernel, mode),
        out_shape=(
            jax.ShapeDtypeStruct((steps * SIDE, HEAD_DIM, rows), jnp.float32),
            jax.ShapeDtypeStruct((steps * SIDE, 8, rows), jnp.float32),
        ),
        grid_spec=pltpu.PrefetchScalarGridSpec(
            num_scalar_prefetch=2,
            grid=(steps,),
            in_specs=in_specs,
            out_specs=(
                pl.BlockSpec((SIDE, HEAD_DIM, rows), lambda i, *_: (i, 0, 0)),
                pl.BlockSpec((SIDE, 8, rows), lambda i, *_: (i, 0, 0)),
            ),
            scratch_shapes=state_shapes(rows, 1),
        ),
        cost_estimate=cost(rows, 1, steps * SIDE),
        name="fold_own" if mode is None else "fold_got",
    )(place, bounds, queries, *pairs)


def merge_kernel(place, own, own_lse, got_l, lse_l, got_r, lse_r, one_ref, two_ref, three_ref, out_ref):
    ctx = place[0] // HEADS_AXIS

    def sent(ref, flag, h):
        tail = ref[h, HEAD_DIM:, :].astype(jnp.float32)
        lse = jnp.where(flag, tail[0:1, :] + tail[1:2, :] + tail[2:3, :], NEG_FILL)
        return jnp.where(flag, ref[h, :HEAD_DIM, :].astype(jnp.float32), 0.0), lse

    def kept(ref, lse_ref, flag, h):
        return jnp.where(flag, ref[h], 0.0), jnp.where(flag, lse_ref[h, 0:1, :], NEG_FILL)

    def combine(others):
        for h in range(SIDE):
            parts = [(own[h], own_lse[h, 0:1, :])] + others(h)
            peak = functools.reduce(jnp.maximum, [lse for _, lse in parts])
            shares = [jnp.exp2(lse - peak) for _, lse in parts]
            inverse = 1.0 / functools.reduce(jnp.add, shares)
            summed = functools.reduce(jnp.add, [out * (share * inverse) for (out, _), share in zip(parts, shares)])
            out_ref[:, cols_of(h)] = summed.astype(out_ref.dtype).T

    @pl.when(pl.program_id(0) == 0)
    def _():
        combine(
            lambda h: [kept(got_l, lse_l, ctx == 1, h), sent(one_ref, ctx >= 2, h), sent(two_ref, ctx == 3, h)]
        )

    @pl.when(pl.program_id(0) == 1)
    def _():
        combine(lambda h: [kept(got_r, lse_r, ctx >= 2, h), sent(three_ref, ctx >= 1, h)])


def merge(place, own, got_l, got_r, one, two, three):
    rows = one.shape[2]
    tall = HEAD_DIM + EXTRA
    moving = lambda i, *_: (i, 0, 0)
    fixed = lambda i, *_: (0, 0, 0)
    pair = lambda at: [pl.BlockSpec((SIDE, HEAD_DIM, rows), at), pl.BlockSpec((SIDE, 8, rows), at)]
    return pl.pallas_call(
        merge_kernel,
        out_shape=jax.ShapeDtypeStruct((rows, 2 * SIDE * HEAD_DIM), jnp.bfloat16),
        grid_spec=pltpu.PrefetchScalarGridSpec(
            num_scalar_prefetch=1,
            grid=(2,),
            in_specs=pair(moving) + pair(fixed) + pair(fixed) + [pl.BlockSpec((SIDE, tall, rows), fixed)] * 3,
            out_specs=pl.BlockSpec((rows, SIDE * HEAD_DIM), lambda i, *_: (0, i)),
        ),
        name="merge",
    )(place, *own, *got_l, *got_r, one, two, three)


def on_device(mix_query, mix_key, mix_value, mr_filter, doc_ids, att_query, att_key, att_value):
    at_ctx = lax.axis_index("ctx")
    at_head = lax.axis_index("head")
    heads = lax.axis_size("head")
    blocks = lax.axis_size("ctx")
    half = SIDE * HEAD_DIM

    def pass_on(x, *pairs):
        return lax.ppermute(x, "ctx", list(pairs))

    pack_l = jnp.stack([att_key[:, :half], att_value[:, :half]])
    pack_r = jnp.stack([att_key[:, half:], att_value[:, half:]])
    query_l, query_r = att_query[:, :half], att_query[:, half:]
    query_x = jnp.where(at_ctx == 3, query_l, query_r)
    pack_l, pack_r, query_l, query_r, query_x, doc_ids, att_query = lax.optimization_barrier(
        (pack_l, pack_r, query_l, query_r, query_x, doc_ids, att_query)
    )
    kv_l = pass_on(pack_l, (0, 1), (1, 0))
    kv_r = pass_on(pack_r, (0, 3), (1, 2))
    q_x = pass_on(query_x, (3, 2), (1, 0))
    q_l = pass_on(query_l, (2, 1), (3, 0))
    q_r = pass_on(query_r, (2, 3), (3, 2))

    place = jnp.reshape(lax.axis_index(("ctx", "head")), (1,)).astype(jnp.int32)
    bounds = jnp.sum((doc_ids[None, :] < jnp.arange(4, dtype=jnp.int32)[:, None]).astype(jnp.int32), axis=1)

    own = fold_keep(None, place, bounds, att_query, att_key, att_value)
    product = (mix_key.astype(jnp.float32) * mix_value.astype(jnp.float32)).astype(jnp.bfloat16)
    own, q_x, q_l, q_r, kv_l, kv_r, product = lax.optimization_barrier((own, q_x, q_l, q_r, kv_l, kv_r, product))
    width = product.shape[1]
    count = blocks * heads
    prod_a, prod_b = product[:, : width // 2], product[:, width // 2 :]
    rim_a = lax.ppermute(prod_a, ("ctx", "head"), [(i, i + 1) for i in range(count - 1)])
    staged = lax.ppermute(
        prod_b, ("ctx", "head"), [(i, i + heads) for i in range(count - heads) if i % heads == heads - 1]
    )
    send_l = fold_send(0, place, bounds, q_l, q_x, att_key, att_value, kv_l)
    part_1 = pass_on(send_l, (1, 2), (0, 3))
    part_2 = pass_on(send_l, (2, 3))
    send_r = fold_send(1, place, bounds, q_r, q_x, att_key, att_value, kv_r)
    part_3 = pass_on(send_r, (0, 1), (3, 2), (2, 3))
    staged, prod_b, send_r, send_l, att_query = lax.optimization_barrier((staged, prod_b, send_r, send_l, att_query))
    rim_b = lax.ppermute(
        jnp.where(at_head == heads - 1, staged, prod_b), "head", [(i, (i + 1) % heads) for i in range(heads)]
    )
    got_l = fold_keep(0, place, bounds, att_query, kv_l)
    got_r = fold_keep(1, place, bounds, att_query, kv_r)
    mixed = mixer(place, bounds, rim_a, rim_b, product, mix_query, mr_filter)
    place, mixed = lax.optimization_barrier((place, mixed))
    attended = merge(place, own, got_l, got_r, part_1, part_2, part_3)
    return (mixed, attended)


def solution(mesh):
    placed = (
        P(("dp", "ctx", "head"), None),
        P(("dp", "ctx", "head"), None),
        P(("dp", "ctx", "head"), None),
        P(),
        P("dp"),
        P(("dp", "ctx"), "head"),
        P(("dp", "ctx"), "head"),
        P(("dp", "ctx"), "head"),
    )
    return jax.shard_map(
        on_device,
        mesh=mesh,
        in_specs=placed,
        out_specs=(P(("dp", "ctx", "head"), None), P(("dp", "ctx"), "head")),
        check_vma=False,
    )
```

time: 194 us -> 102 us (0.53)
  matrix products: 83.6 us -> 0 us
  Pallas kernels: 0 us -> 37.2 us
  local copies, waits for them, and re-layouts: 41.3 us -> 5.12 us
  starting transfers between devices: 2 us -> 29.7 us
  other arithmetic: 26.9 us -> 4.12 us
  between operations: 14.1 us -> 0.82 us
  waiting for transfers between devices: 17.5 us -> 23.3 us
  loops' own time: 5.79 us -> 0 us
    dot_general x24 -> x0, matrix products: 83.6 us -> none  [the longest x8 37.5 us: toeplitz_rows(): jnp.dot(filters, table, preferred_element_type=jnp.float32)]
    pallas_call x0 -> x7, Pallas kernels: none -> 37.2 us  [the longest x3 14.6 us: fold_keep(): pl.pallas_call(functools.partial(keep_kernel, mode), out_shape=(jax.Shape...]
    ppermute x1 -> x11, starting transfers between devices: 1.92 us -> 29.7 us  [the longest x8 22.8 us: pass_on(): return lax.ppermute(x, 'ctx', list(pairs))]
    unnamed x14 -> x24, local copies, waits for them, and re-layouts: 11.9 us -> 1.5 us
    while x28 -> x0, local copies, waits for them, and re-layouts: 9.53 us -> none
    reduce_sum x4 -> x1, other arithmetic: 8.13 us -> 0.8 us  [on_device(): jnp.sum((doc_ids[None, :] < jnp.arange(4, dtype=jnp.int32)[:, None]).asty...]
    dynamic_slice x10 -> x0, local copies, waits for them, and re-layouts: 7.23 us -> none  [the longest x4 6.77 us: visit_block(): lax.dynamic_slice_in_dim(value_piece, block_at * block_len, block_len, 0)]
    ppermute x1 -> x11, waiting for transfers between devices: 17.5 us -> 23.3 us  [the longest x8 23.3 us: pass_on(): return lax.ppermute(x, 'ctx', list(pairs))]
  transfers between devices with their start and end apart: 3 -> 11, of which waited for: 1 -> 3; matrix products, arithmetic and copies ran while one was open for 55% -> 1% of each run, Pallas kernels for 0% -> 33%
where the time goes in v1:
time: 102 us; the launch traced here: 100 us
  Pallas kernels  37.2 us (36%)
  starting transfers between devices  29.7 us (29%)
  waiting for transfers between devices  23.3 us (23%)
  local copies, waits for them, and re-layouts  5.12 us (5%)
  other arithmetic  4.12 us (4%)
    ppermute x8, waiting for transfers between devices, pass_on(): return lax.ppermute(x, 'ctx', list(pairs))  23.3 us
    ppermute x8, starting transfers between devices, pass_on(): return lax.ppermute(x, 'ctx', list(pairs))  22.8 us
    pallas_call x3, Pallas kernels, fold_keep(): pl.pallas_call(functools.partial(keep_kernel, mode), out_shape=(jax.Shape...  14.6 us
    pallas_call x1, Pallas kernels, mixer(): pl.pallas_call(functools.partial(conv_kernel, group_size), out_shape=jax....  11.2 us
    pallas_call x2, Pallas kernels, fold_send(): pl.pallas_call(functools.partial(send_kernel, side), out_shape=jax.ShapeD...  7.12 us
    ppermute x1, starting transfers between devices, on_device(): lax.ppermute(jnp.where(at_head == heads - 1, staged, prod_b), 'head', [(i...  4.29 us
    pallas_call x1, Pallas kernels, merge(): pl.pallas_call(merge_kernel, out_shape=jax.ShapeDtypeStruct((rows, 2 * SI...  4.21 us
    another operation x2, local copies, waits for them, and re-layouts, on_device(): pack_r = jnp.stack([att_key[:, half:], att_value[:, half:]])  2.46 us
  transfers between devices with their start and end apart: 11, of which 3 were waited for; matrix products, arithmetic and copies ran while one was open for 1% of the time, Pallas kernels for 33%

profile of v1, /device:TPU:118, one launch (start us, length us, event | category | flops | bytes accessed | tf_op | source)
XLA Modules:
  0.0 100.3 jit_solution(8784142994772013897)
XLA Ops:
  0.6 0.0 copy-start
  0.6 0.0 copy-start.1
  0.7 1.4 %slice_bitcast_fusion = (bf16[1,512,512]{2,1,0:T(8,128)(2,1)S(1)}, bf16[1,512,512]{2,1,0:T(8,128)(2,1)S(1)}) fusion(bf16[512,1024]{1,0:T(8,128)(2,1)} %v_ref.3), kind=kLoop, calls=%fused_computation.4 | loop fusion | bytes 2097152 | tf_op jit(solution)/shard_map/stack | solution.py:328
  2.1 0.1 copy-done
  2.2 1.0 %slice_bitcast_fusion.1 = (bf16[1,512,512]{2,1,0:T(8,128)(2,1)}, bf16[1,512,512]{2,1,0:T(8,128)(2,1)}) fusion(bf16[512,1024]{1,0:T(8,128)(2,1)S(1)} %copy-done), kind=kLoop, calls=%fused_computation.5 | loop fusion | bytes 2097152 | tf_op jit(solution)/shard_map/stack | solution.py:328
  3.2 0.0 copy-start.6
  3.2 0.0 copy-start.7
  3.2 0.0 copy-done.1
  3.2 1.2 %broadcast_select_fusion.1 = (bf16[512,512]{1,0:T(8,128)(2,1)}, bf16[512,512]{1,0:T(8,128)(2,1)}, bf16[512,512]{1,0:T(8,128)(2,1)}) fusion(pred[]{:T(512)S(6)} %eq.6, bf16[512,1024]{1,0:T(8,128)(2,1)S(1)} %copy-done.1), kind=kLoop, calls=%fused_computation.8 | loop fusion | flops 262144 | bytes 2621441 | tf_op jit(solution)/shard_map/jit(_where)/select_n | solution.py:330
  4.4 0.0 copy-done.6
  4.4 0.5 copy-done.7
  5.0 0.0 copy-start.4
  5.0 0.0 copy-start.5
  5.0 1.5 %pad_maximum_fusion = (bf16[2,512,512]{2,1,0:T(8,128)(2,1)}, bf16[2,512,512]{2,1,0:T(8,128)(2,1)}) fusion(bf16[1,512,512]{2,1,0:T(8,128)(2,1)S(1)} %get-tuple-element.62, bf16[1,512,512]{2,1,0:T(8,128)(2,1)S(1)} %copy-done.7, bf16[1,512,512]{2,1,0:T(8,128)(2,1)S(1)} %get-tuple-element.61, bf16[1,512,512]{2,1,0:T(8,128)(2,1)S(1)} %copy-done.6), kind=kLoop, calls=%fused_computation.1 | loop fusion | flops 1048576 | bytes 4194304 | tf_op jit(solution)/shard_map/stack | solution.py:327
  6.5 0.0 copy-start.11
  6.5 3.7 %collective-permute-start = (bf16[512,512]{1,0:T(8,128)(2,1)}, bf16[512,512]{1,0:T(8,128)(2,1)}, u32[]{:S(2)}, u32[]{:S(2)}) collective-permute-start(bf16[512,512]{1,0:T(8,128)(2,1)} %get-tuple-element.32), channel_id=1, source_target_pairs={{12,8},{4,0},{13,9},{5,1},{14,10},{6,2},{15,11},{7,3},{28,24},{20,... | collective-permute-start | bytes 1572872 | tf_op jit(solution)/shard_map/ppermute | solution.py:325
  10.2 2.1 %collective-permute-start.1 = (bf16[512,512]{1,0:T(8,128)(2,1)}, bf16[512,512]{1,0:T(8,128)(2,1)}, u32[]{:S(2)}, u32[]{:S(2)}) collective-permute-start(bf16[512,512]{1,0:T(8,128)(2,1)} %get-tuple-element.33), channel_id=1, source_target_pairs={{8,4},{12,0},{9,5},{13,1},{10,6},{14,2},{11,7},{15,3},{24,20},{28,... | collective-permute-start | bytes 1572872 | tf_op jit(solution)/shard_map/ppermute | solution.py:325
  12.3 3.6 %collective-permute-start.2 = (bf16[512,512]{1,0:T(8,128)(2,1)}, bf16[512,512]{1,0:T(8,128)(2,1)}, u32[]{:S(2)}, u32[]{:S(2)}) collective-permute-start(bf16[512,512]{1,0:T(8,128)(2,1)} %get-tuple-element.34), channel_id=1, source_target_pairs={{8,12},{12,8},{9,13},{13,9},{10,14},{14,10},{11,15},{15,11},{24,28... | collective-permute-start | bytes 1572872 | tf_op jit(solution)/shard_map/ppermute | solution.py:325
  15.9 0.7 collective-permute-start.3
  16.6 1.3 %collective-permute-start.4 = (bf16[2,512,512]{2,1,0:T(8,128)(2,1)}, bf16[2,512,512]{2,1,0:T(8,128)(2,1)}, u32[]{:S(2)}, u32[]{:S(2)}) collective-permute-start(bf16[2,512,512]{2,1,0:T(8,128)(2,1)} %get-tuple-element.36), channel_id=1, source_target_pairs={{0,12},{4,8},{1,13},{5,9},{2,14},{6,10},{3,15},{7,11},{16,28},{20,... | collective-permute-start | bytes 3145736 | tf_op jit(solution)/shard_map/ppermute | solution.py:325
  17.9 0.0 copy-done.4
  17.9 0.0 copy-done.5
  17.9 0.5 multiply_convert_fusion.prod_ref
  18.4 0.0 copy-start.2
  18.4 0.0 copy-done.11
  18.4 0.8 convert_reduce_fusion.bounds
  19.2 8.2 %fold_own.1 = (f32[8,128,512]{2,1,0:T(8,128)}, f32[8,8,512]{2,1,0:T(8,128)}) custom-call(s32[1]{0:T(128)} %bitcast.place, s32[4]{0:T(128)} %convert_reduce_fusion.bounds, bf16[512,1024]{1,0:T(8,128)(2,1)} %q_ref.2, bf16[512,1024]{1,0:T(8,128)(2,1)} %k_ref.3, bf16[512,1024]{1,0:T(8,128)(2,1)} %v_ref.3), custom_call_target="tpu_custom_call" | custom-call | flops 1 | bytes 1 | tf_op jit(solution)/shard_map/fold_own/pallas_call | solution.py:246
  27.4 0.0 collective-permute-done.qb_ref
  27.4 0.0 collective-permute-done.1.qa_ref
  27.4 4.6 %collective-permute-done.2.qa_ref = bf16[512,512]{1,0:T(8,128)(2,1)} collective-permute-done((bf16[512,512]{1,0:T(8,128)(2,1)}, bf16[512,512]{1,0:T(8,128)(2,1)}, u32[]{:S(2)}, u32[]{:S(2)}) %collective-permute-start.2) | collective-permute-done | bytes 524320 | tf_op jit(solution)/shard_map/ppermute | solution.py:325
  32.1 0.0 collective-permute-done.3.kv_ref.rest_0_
  32.1 0.0 copy-start.3
  32.1 12.0 %collective-permute-done.4.kv_ref.rest_0_ = bf16[2,512,512]{2,1,0:T(8,128)(2,1)} collective-permute-done((bf16[2,512,512]{2,1,0:T(8,128)(2,1)}, bf16[2,512,512]{2,1,0:T(8,128)(2,1)}, u32[]{:S(2)}, u32[]{:S(2)}) %collective-permute-start.4) | collective-permute-done | bytes 1048608 | tf_op jit(solution)/shard_map/ppermute | solution.py:325
  44.1 0.0 copy-done.3
  44.1 1.2 %fusion = (bf16[128,4096]{1,0:T(8,128)(2,1)S(1)}, bf16[128,4096]{1,0:T(8,128)(2,1)}) fusion(bf16[128,8192]{1,0:T(8,128)(2,1)S(1)} %multiply_convert_fusion.prod_ref), kind=kLoop, calls=%fused_computation.11 | loop fusion | bytes 4194304 | tf_op jit(solution)/shard_map/slice | solution.py:348
  45.2 0.0 copy-done.2
  45.2 0.7 collective-permute-start.6
  46.0 1.9 %collective-permute-start.5 = (bf16[128,4096]{1,0:T(8,128)(2,1)}, bf16[128,4096]{1,0:T(8,128)(2,1)}, u32[]{:S(2)}, u32[]{:S(2)}) collective-permute-start(bf16[128,4096]{1,0:T(8,128)(2,1)} %get-tuple-element.55), channel_id=1, source_target_pairs={{0,1},{1,2},{2,3},{3,4},{4,5},{5,6},{6,7},{7,8},{8,9},{9,10},{10,1... | collective-permute-start | bytes 3145736 | tf_op jit(solution)/shard_map/ppermute | solution.py:349
  47.9 3.8 %fold_send.2 = bf16[4,144,512]{2,1,0:T(8,128)(2,1)} custom-call(s32[1]{0:T(128)} %bitcast.place, s32[4]{0:T(128)} %convert_reduce_fusion.bounds, bf16[512,512]{1,0:T(8,128)(2,1)} %collective-permute-done.2.qa_ref, bf16[512,512]{1,0:T(8,128)(2,1)} %collective-permute-done.qb_ref, bf16[512,1024]{1,0:T(8,128)(2,1)} %k_ref.3, bf16[512,1024]{1,0:T(8,128)(2,1)} %v_ref.3, ...), custom_call_target="tpu_custom_call" | custom-call | flops 1 | bytes 1 | tf_op jit(solution)/shard_map/fold_send/pallas_call | solution.py:219
  51.7 3.4 %fold_send.3 = bf16[4,144,512]{2,1,0:T(8,128)(2,1)} custom-call(s32[1]{0:T(128)} %bitcast.place, s32[4]{0:T(128)} %convert_reduce_fusion.bounds, bf16[512,512]{1,0:T(8,128)(2,1)} %collective-permute-done.1.qa_ref, bf16[512,512]{1,0:T(8,128)(2,1)} %collective-permute-done.qb_ref, bf16[512,1024]{1,0:T(8,128)(2,1)} %k_ref.3, bf16[512,1024]{1,0:T(8,128)(2,1)} %v_ref.3, ...), custom_call_target="tpu_custom_call" | custom-call | flops 1 | bytes 1 | tf_op jit(solution)/shard_map/fold_send/pallas_call | solution.py:219
  55.0 0.0 collective-permute-done.6
  55.0 0.1 broadcast_select_fusion
  55.1 4.3 %collective-permute-start.7 = (bf16[128,4096]{1,0:T(8,128)(2,1)S(1)}, bf16[128,4096]{1,0:T(8,128)(2,1)}, u32[]{:S(2)}, u32[]{:S(2)}) collective-permute-start(bf16[128,4096]{1,0:T(8,128)(2,1)S(1)} %broadcast_select_fusion), channel_id=1, source_target_pairs={{0,1},{1,2},{2,3},{3,0},{4,5},{5,6},{6,7},{7,4},{8,9},{9,10},{10,1... | collective-permute-start | bytes 3145736 | tf_op jit(solution)/shard_map/ppermute | solution.py:359
  59.4 1.3 %collective-permute-start.8 = (bf16[4,144,512]{2,1,0:T(8,128)(2,1)}, bf16[4,144,512]{2,1,0:T(8,128)(2,1)S(1)}, u32[]{:S(2)}, u32[]{:S(2)}) collective-permute-start(bf16[4,144,512]{2,1,0:T(8,128)(2,1)} %fold_send.3), channel_id=1, source_target_pairs={{4,8},{0,12},{5,9},{1,13},{6,10},{2,14},{7,11},{3,15},{20,24},{16,... | collective-permute-start | bytes 1769480 | tf_op jit(solution)/shard_map/ppermute | solution.py:325
  60.7 1.3 %collective-permute-start.9 = (bf16[4,144,512]{2,1,0:T(8,128)(2,1)}, bf16[4,144,512]{2,1,0:T(8,128)(2,1)S(1)}, u32[]{:S(2)}, u32[]{:S(2)}) collective-permute-start(bf16[4,144,512]{2,1,0:T(8,128)(2,1)} %fold_send.3), channel_id=1, source_target_pairs={{8,12},{9,13},{10,14},{11,15},{24,28},{25,29},{26,30},{27,31},{40,... | collective-permute-start | bytes 1769480 | tf_op jit(solution)/shard_map/ppermute | solution.py:325
  62.0 8.8 %collective-permute-start.10 = (bf16[4,144,512]{2,1,0:T(8,128)(2,1)}, bf16[4,144,512]{2,1,0:T(8,128)(2,1)S(1)}, u32[]{:S(2)}, u32[]{:S(2)}) collective-permute-start(bf16[4,144,512]{2,1,0:T(8,128)(2,1)} %fold_send.2), channel_id=1, source_target_pairs={{0,4},{12,8},{8,12},{1,5},{13,9},{9,13},{2,6},{14,10},{10,14},{3,7... | collective-permute-start | bytes 1769480 | tf_op jit(solution)/shard_map/ppermute | solution.py:325
  70.8 3.0 %fold_got.2 = (f32[4,128,512]{2,1,0:T(8,128)}, f32[4,8,512]{2,1,0:T(8,128)}) custom-call(s32[1]{0:T(128)} %bitcast.place, s32[4]{0:T(128)} %convert_reduce_fusion.bounds, bf16[512,1024]{1,0:T(8,128)(2,1)} %q_ref.2, bf16[2,512,512]{2,1,0:T(8,128)(2,1)} %copy-done.3), custom_call_target="tpu_custom_call" | custom-call | flops 1 | bytes 1 | tf_op jit(solution)/shard_map/fold_got/pallas_call | solution.py:246
  73.9 3.4 %fold_got.3 = (f32[4,128,512]{2,1,0:T(8,128)}, f32[4,8,512]{2,1,0:T(8,128)}) custom-call(s32[1]{0:T(128)} %bitcast.place, s32[4]{0:T(128)} %convert_reduce_fusion.bounds, bf16[512,1024]{1,0:T(8,128)(2,1)} %q_ref.2, bf16[2,512,512]{2,1,0:T(8,128)(2,1)} %collective-permute-done.4.kv_ref.rest_0_), custom_call_target="tpu_custom_call" | custom-call | flops 1 | bytes 1 | tf_op jit(solution)/shard_map/fold_got/pallas_call | solution.py:246
  77.3 0.0 collective-permute-done.5.rim_a_ref
  77.3 0.0 collective-permute-done.7.rim_b_ref
  77.3 11.2 %mixer.1 = bf16[128,8192]{1,0:T(8,128)(2,1)} custom-call(s32[1]{0:T(128)} %bitcast.place, s32[4]{0:T(128)} %convert_reduce_fusion.bounds, bf16[128,4096]{1,0:T(8,128)(2,1)} %collective-permute-done.5.rim_a_ref, bf16[128,4096]{1,0:T(8,128)(2,1)} %collective-permute-done.7.rim_b_ref, bf16[128,8192]{1,0:T(8,128)(2,1)} %copy-done.2, ...), custom_call_target="tpu_custom_call" | custom-call | flops 8589934592 | bytes 8388608 | tf_op jit(solution)/shard_map/mixer/pallas_call | solution.py:68
  88.5 0.0 collective-permute-done.8.one_ref
  88.5 0.0 copy-start.8
  88.5 0.0 collective-permute-done.9.two_ref
  88.6 0.0 copy-start.9
  88.6 6.7 %collective-permute-done.10.three_ref = bf16[4,144,512]{2,1,0:T(8,128)(2,1)S(1)} collective-permute-done((bf16[4,144,512]{2,1,0:T(8,128)(2,1)}, bf16[4,144,512]{2,1,0:T(8,128)(2,1)S(1)}, u32[]{:S(2)}, u32[]{:S(2)}) %collective-permute-start.10) | collective-permute-done | bytes 589856 | tf_op jit(solution)/shard_map/ppermute | solution.py:325
  95.2 0.0 copy-start.10
  95.2 0.0 copy-done.8
  95.2 0.0 copy-done.9
  95.2 0.8 copy-done.10
  96.1 4.2 %merge.1 = bf16[512,1024]{1,0:T(8,128)(2,1)} custom-call(s32[1]{0:T(128)} %bitcast.place, f32[8,128,512]{2,1,0:T(8,128)} %get-tuple-element.47.own, f32[8,8,512]{2,1,0:T(8,128)} %get-tuple-element.48.own_lse, f32[4,128,512]{2,1,0:T(8,128)} %get-tuple-element.50.got_l, f32[4,8,512]{2,1,0:T(8,128)} %get-tuple-element.51.lse_l, ...), custom_call_target="tpu_custom_call" | custom-call | tf_op jit(solution)/shard_map/merge/pallas_call | solution.py:304
Async XLA Ops:
  0.6 1.5 %copy-start = (bf16[512,1024]{1,0:T(8,128)(2,1)S(1)}, bf16[512,1024]{1,0:T(8,128)(2,1)}, u32[]{:S(2)}) copy-start(bf16[512,1024]{1,0:T(8,128)(2,1)} %k_ref.3) | copy-start | bytes 3145732
  0.6 2.6 %copy-start.1 = (bf16[512,1024]{1,0:T(8,128)(2,1)S(1)}, bf16[512,1024]{1,0:T(8,128)(2,1)}, u32[]{:S(2)}) copy-start(bf16[512,1024]{1,0:T(8,128)(2,1)} %q_ref.2) | copy-start | bytes 3145732
  3.2 1.2 %copy-start.6 = (bf16[1,512,512]{2,1,0:T(8,128)(2,1)S(1)}, bf16[1,512,512]{2,1,0:T(8,128)(2,1)}, u32[]{:S(2)}) copy-start(bf16[1,512,512]{2,1,0:T(8,128)(2,1)} %get-tuple-element.59) | copy-start | bytes 1572868
  3.2 1.8 %copy-start.7 = (bf16[1,512,512]{2,1,0:T(8,128)(2,1)S(1)}, bf16[1,512,512]{2,1,0:T(8,128)(2,1)}, u32[]{:S(2)}) copy-start(bf16[1,512,512]{2,1,0:T(8,128)(2,1)} %get-tuple-element.60) | copy-start | bytes 1572868
  5.0 12.9 %copy-start.4 = (bf16[128,8192]{1,0:T(8,128)(2,1)S(1)}, bf16[128,8192]{1,0:T(8,128)(2,1)}, u32[]{:S(2)}) copy-start(bf16[128,8192]{1,0:T(8,128)(2,1)} %param.10) | copy-start | bytes 6291460
  5.0 12.9 %copy-start.5 = (bf16[128,8192]{1,0:T(8,128)(2,1)S(1)}, bf16[128,8192]{1,0:T(8,128)(2,1)}, u32[]{:S(2)}) copy-start(bf16[128,8192]{1,0:T(8,128)(2,1)} %param.9) | copy-start | bytes 6291460
  6.5 11.9 %copy-start.11 = (s32[2048]{0:T(1024)S(1)}, s32[2048]{0:T(1024)}, u32[]{:S(2)}) copy-start(s32[2048]{0:T(1024)} %param.12) | copy-start | bytes 24580
  6.5 20.9 %collective-permute-start = (bf16[512,512]{1,0:T(8,128)(2,1)}, bf16[512,512]{1,0:T(8,128)(2,1)}, u32[]{:S(2)}, u32[]{:S(2)}) collective-permute-start(bf16[512,512]{1,0:T(8,128)(2,1)} %get-tuple-element.32), channel_id=1, source_target_pairs={{12,8},{4,0},{13,9},{5,1},{14,10},{6,2},{15,11},{7,3},{28,24},{20,... | collective-permute-start | bytes 1572872 | tf_op jit(solution)/shard_map/ppermute | solution.py:325
  10.2 17.3 %collective-permute-start.1 = (bf16[512,512]{1,0:T(8,128)(2,1)}, bf16[512,512]{1,0:T(8,128)(2,1)}, u32[]{:S(2)}, u32[]{:S(2)}) collective-permute-start(bf16[512,512]{1,0:T(8,128)(2,1)} %get-tuple-element.33), channel_id=1, source_target_pairs={{8,4},{12,0},{9,5},{13,1},{10,6},{14,2},{11,7},{15,3},{24,20},{28,... | collective-permute-start | bytes 1572872 | tf_op jit(solution)/shard_map/ppermute | solution.py:325
  12.3 19.8 %collective-permute-start.2 = (bf16[512,512]{1,0:T(8,128)(2,1)}, bf16[512,512]{1,0:T(8,128)(2,1)}, u32[]{:S(2)}, u32[]{:S(2)}) collective-permute-start(bf16[512,512]{1,0:T(8,128)(2,1)} %get-tuple-element.34), channel_id=1, source_target_pairs={{8,12},{12,8},{9,13},{13,9},{10,14},{14,10},{11,15},{15,11},{24,28... | collective-permute-start | bytes 1572872 | tf_op jit(solution)/shard_map/ppermute | solution.py:325
  15.9 16.2 %collective-permute-start.3 = (bf16[2,512,512]{2,1,0:T(8,128)(2,1)}, bf16[2,512,512]{2,1,0:T(8,128)(2,1)S(1)}, u32[]{:S(2)}, u32[]{:S(2)}) collective-permute-start(bf16[2,512,512]{2,1,0:T(8,128)(2,1)} %get-tuple-element.35), channel_id=1, source_target_pairs={{0,4},{4,0},{1,5},{5,1},{2,6},{6,2},{3,7},{7,3},{16,20},{20,16},{1... | collective-permute-start | bytes 3145736 | tf_op jit(solution)/shard_map/ppermute | solution.py:325
  16.6 27.5 %collective-permute-start.4 = (bf16[2,512,512]{2,1,0:T(8,128)(2,1)}, bf16[2,512,512]{2,1,0:T(8,128)(2,1)}, u32[]{:S(2)}, u32[]{:S(2)}) collective-permute-start(bf16[2,512,512]{2,1,0:T(8,128)(2,1)} %get-tuple-element.36), channel_id=1, source_target_pairs={{0,12},{4,8},{1,13},{5,9},{2,14},{6,10},{3,15},{7,11},{16,28},{20,... | collective-permute-start | bytes 3145736 | tf_op jit(solution)/shard_map/ppermute | solution.py:325
  18.4 26.8 %copy-start.2 = (bf16[128,8192]{1,0:T(8,128)(2,1)}, bf16[128,8192]{1,0:T(8,128)(2,1)S(1)}, u32[]{:S(2)}) copy-start(bf16[128,8192]{1,0:T(8,128)(2,1)S(1)} %multiply_convert_fusion.prod_ref) | copy-start | bytes 6291460
  32.1 12.0 %copy-start.3 = (bf16[2,512,512]{2,1,0:T(8,128)(2,1)}, bf16[2,512,512]{2,1,0:T(8,128)(2,1)S(1)}, u32[]{:S(2)}) copy-start(bf16[2,512,512]{2,1,0:T(8,128)(2,1)S(1)} %collective-permute-done.3.kv_ref.rest_0_) | copy-start | bytes 3145732
  45.2 9.8 %collective-permute-start.6 = (bf16[128,4096]{1,0:T(8,128)(2,1)S(1)}, bf16[128,4096]{1,0:T(8,128)(2,1)S(1)}, u32[]{:S(2)}, u32[]{:S(2)}) collective-permute-start(bf16[128,4096]{1,0:T(8,128)(2,1)S(1)} %get-tuple-element.44), channel_id=1, source_target_pairs={{3,7},{7,11},{11,15},{19,23},{23,27},{27,31},{35,39},{39,43},{43,4... | collective-permute-start | bytes 3145736 | tf_op jit(solution)/shard_map/ppermute | solution.py:350
  46.0 31.3 %collective-permute-start.5 = (bf16[128,4096]{1,0:T(8,128)(2,1)}, bf16[128,4096]{1,0:T(8,128)(2,1)}, u32[]{:S(2)}, u32[]{:S(2)}) collective-permute-start(bf16[128,4096]{1,0:T(8,128)(2,1)} %get-tuple-element.55), channel_id=1, source_target_pairs={{0,1},{1,2},{2,3},{3,4},{4,5},{5,6},{6,7},{7,8},{8,9},{9,10},{10,1... | collective-permute-start | bytes 3145736 | tf_op jit(solution)/shard_map/ppermute | solution.py:349
  55.1 22.2 %collective-permute-start.7 = (bf16[128,4096]{1,0:T(8,128)(2,1)S(1)}, bf16[128,4096]{1,0:T(8,128)(2,1)}, u32[]{:S(2)}, u32[]{:S(2)}) collective-permute-start(bf16[128,4096]{1,0:T(8,128)(2,1)S(1)} %broadcast_select_fusion), channel_id=1, source_target_pairs={{0,1},{1,2},{2,3},{3,0},{4,5},{5,6},{6,7},{7,4},{8,9},{9,10},{10,1... | collective-permute-start | bytes 3145736 | tf_op jit(solution)/shard_map/ppermute | solution.py:359
  59.4 29.1 %collective-permute-start.8 = (bf16[4,144,512]{2,1,0:T(8,128)(2,1)}, bf16[4,144,512]{2,1,0:T(8,128)(2,1)S(1)}, u32[]{:S(2)}, u32[]{:S(2)}) collective-permute-start(bf16[4,144,512]{2,1,0:T(8,128)(2,1)} %fold_send.3), channel_id=1, source_target_pairs={{4,8},{0,12},{5,9},{1,13},{6,10},{2,14},{7,11},{3,15},{20,24},{16,... | collective-permute-start | bytes 1769480 | tf_op jit(solution)/shard_map/ppermute | solution.py:325
  60.7 27.8 %collective-permute-start.9 = (bf16[4,144,512]{2,1,0:T(8,128)(2,1)}, bf16[4,144,512]{2,1,0:T(8,128)(2,1)S(1)}, u32[]{:S(2)}, u32[]{:S(2)}) collective-permute-start(bf16[4,144,512]{2,1,0:T(8,128)(2,1)} %fold_send.3), channel_id=1, source_target_pairs={{8,12},{9,13},{10,14},{11,15},{24,28},{25,29},{26,30},{27,31},{40,... | collective-permute-start | bytes 1769480 | tf_op jit(solution)/shard_map/ppermute | solution.py:325
  62.0 33.2 %collective-permute-start.10 = (bf16[4,144,512]{2,1,0:T(8,128)(2,1)}, bf16[4,144,512]{2,1,0:T(8,128)(2,1)S(1)}, u32[]{:S(2)}, u32[]{:S(2)}) collective-permute-start(bf16[4,144,512]{2,1,0:T(8,128)(2,1)} %fold_send.2), channel_id=1, source_target_pairs={{0,4},{12,8},{8,12},{1,5},{13,9},{9,13},{2,6},{14,10},{10,14},{3,7... | collective-permute-start | bytes 1769480 | tf_op jit(solution)/shard_map/ppermute | solution.py:325
  88.5 6.7 %copy-start.8 = (bf16[4,144,512]{2,1,0:T(8,128)(2,1)}, bf16[4,144,512]{2,1,0:T(8,128)(2,1)S(1)}, u32[]{:S(2)}) copy-start(bf16[4,144,512]{2,1,0:T(8,128)(2,1)S(1)} %collective-permute-done.8.one_ref) | copy-start | bytes 1769476
  88.6 6.7 %copy-start.9 = (bf16[4,144,512]{2,1,0:T(8,128)(2,1)}, bf16[4,144,512]{2,1,0:T(8,128)(2,1)S(1)}, u32[]{:S(2)}) copy-start(bf16[4,144,512]{2,1,0:T(8,128)(2,1)S(1)} %collective-permute-done.9.two_ref) | copy-start | bytes 1769476
  95.2 0.8 copy-start.10

commit v2 on v1

v2 whole, which is shorter than its diff:
```python
import functools
import math

import jax
import jax.numpy as jnp
from jax import lax
from jax.experimental import pallas as pl
from jax.experimental.pallas import tpu as pltpu
from jax.sharding import PartitionSpec as P

HEAD_DIM = 128
NEG_FILL = -1e30
LOG2_SCALE = math.log2(math.e) / math.sqrt(HEAD_DIM)
SIDE = 4
SUB = 256
EXTRA = 16
COLS = 2048
HEADS_AXIS = 4


def pick(at, *values):
    out = jnp.int32(values[-1])
    for i in range(len(values) - 2, -1, -1):
        out = jnp.where(at == i, jnp.int32(values[i]), out)
    return out


def first_of(bounds, position):
    first = jnp.zeros_like(position)
    for doc in range(1, 4):
        first = jnp.where(bounds[doc] <= position, bounds[doc], first)
    return first


def conv_kernel(group_size, place, bounds, rim_a_ref, rim_b_ref, prod_ref, query_ref, filt_ref, out_ref, mask):
    rows, cols = prod_ref.shape
    step = pl.program_id(0)

    @pl.when(step == 0)
    def _():
        token = place[0] * rows + lax.broadcasted_iota(jnp.int32, (2 * rows, rows), 1)
        source = (place[0] - 1) * rows + lax.broadcasted_iota(jnp.int32, (2 * rows, rows), 0)
        allowed = (source <= token) & (source > token - rows) & (source >= first_of(bounds, token))
        mask[...] = jnp.where(allowed, 1.0, 0.0).astype(jnp.bfloat16)

    rim = jnp.where(step < pl.num_programs(0) // 2, rim_a_ref[...], rim_b_ref[...])
    turned = jnp.concatenate([rim, prod_ref[...]], axis=0).T
    filters = filt_ref[...].astype(jnp.float32)
    allowed = mask[...]
    parts = []
    for g in range(cols // group_size):
        line = jnp.broadcast_to(filters[g : g + 1, :], (rows, rows))
        ring = pltpu.roll(line, 0, 1, stride=1, stride_axis=0).astype(jnp.bfloat16)
        taps = jnp.concatenate([ring, ring], axis=0) * allowed
        parts.append(
            jnp.dot(turned[g * group_size : (g + 1) * group_size], taps, preferred_element_type=jnp.float32)
        )
    total = jnp.concatenate(parts, axis=0).T
    out_ref[...] = (query_ref[...].astype(jnp.float32) * total).astype(out_ref.dtype)


def mixer(place, bounds, rim_a, rim_b, product, mix_query, mr_filter):
    rows, width = product.shape
    groups, filt_len = mr_filter.shape
    group_size = width // groups
    steps = width // COLS
    tile = pl.BlockSpec((rows, COLS), lambda i, *_: (0, i))
    return pl.pallas_call(
        functools.partial(conv_kernel, group_size),
        out_shape=jax.ShapeDtypeStruct((rows, width), jnp.bfloat16),
        grid_spec=pltpu.PrefetchScalarGridSpec(
            num_scalar_prefetch=2,
            grid=(steps,),
            in_specs=[
                pl.BlockSpec((rows, COLS), lambda i, *_: (0, jnp.minimum(i, steps // 2 - 1))),
                pl.BlockSpec((rows, COLS), lambda i, *_: (0, jnp.maximum(i - steps // 2, 0))),
                tile,
                tile,
                pl.BlockSpec((COLS // group_size, filt_len), lambda i, *_: (i, 0)),
            ],
            out_specs=tile,
            scratch_shapes=[pltpu.VMEM((2 * rows, rows), jnp.bfloat16)],
        ),
        cost_estimate=pl.CostEstimate(
            flops=2 * rows * 2 * filt_len * width * 16, bytes_accessed=8 * rows * width, transcendentals=0
        ),
        name="mixer",
    )(place, bounds, rim_a, rim_b, product, mix_query, mr_filter)


def cols_of(h):
    return slice(h * HEAD_DIM, (h + 1) * HEAD_DIM)


def fold_tiles(bounds, query_block, query, sources, heads, state, finish, tile=2 * SUB, turn=None):
    top, den, acc, turned_q, turned_v = state
    rows = query.shape[0]
    turned_q[...] = query.T
    whole_lowest = first_of(bounds, query_block * rows)
    for n, (block, _, value_of) in enumerate(sources):

        inside = (block >= 0) & (block <= query_block) & ((block + 1) * rows > whole_lowest)

        @pl.when(inside if turn is None else turn)
        def _(n=n, value_of=value_of):
            turned_v[n] = value_of().T

    for part in range(rows // SUB):
        at = pl.ds(part * SUB, SUB)
        query_from = query_block * rows + part * SUB
        line_pos = query_from + lax.broadcasted_iota(jnp.int32, (1, SUB), 1)
        first_row = first_of(bounds, line_pos)
        lowest = first_of(bounds, query_from)
        top[...] = jnp.full(top.shape, 0.5 * NEG_FILL, jnp.float32)
        den[...] = jnp.zeros(den.shape, jnp.float32)
        acc[...] = jnp.zeros(acc.shape, jnp.float32)
        for n, (block, key_of, _) in enumerate(sources):
            for piece in range(rows // tile):
                key_from = block * rows + piece * tile
                needed = (block >= 0) & (key_from <= query_from) & (key_from + tile > lowest)

                @pl.when(needed)
                def _(n=n, key_of=key_of, piece=piece, key_from=key_from):
                    take = pl.ds(piece * tile, tile)
                    key_pos = key_from + lax.broadcasted_iota(jnp.int32, (tile, SUB), 0)
                    allowed = (key_pos <= line_pos) & (key_pos >= first_row)
                    scores = [
                        jnp.dot(key_of(h, take), turned_q[cols_of(h), at], preferred_element_type=jnp.float32)
                        for h in range(heads)
                    ]
                    ready = []
                    for h in range(heads):
                        masked = jnp.where(allowed, scores[h], NEG_FILL)
                        old = top[h]
                        new = jnp.maximum(old, jnp.max(masked, axis=0, keepdims=True))
                        weights = jnp.exp2((masked - new) * LOG2_SCALE)
                        factor = jnp.exp2((old - new) * LOG2_SCALE)
                        den[h] = den[h] * factor + jnp.sum(weights, axis=0, keepdims=True)
                        top[h] = new
                        ready.append((weights.astype(jnp.bfloat16), factor))
                    for h, (weights, factor) in enumerate(ready):
                        acc[h] = acc[h] * factor + jnp.dot(
                            turned_v[n, cols_of(h), take], weights, preferred_element_type=jnp.float32
                        )

        for h in range(heads):
            some = den[h] > 0.0
            safe = jnp.where(some, den[h], 1.0)
            lse = jnp.where(some, top[h] * LOG2_SCALE + jnp.log2(safe), NEG_FILL)
            finish(h, at, acc[h] / safe, lse)


def write_message(out_ref, h, at, scaled, lse):
    out_ref[h, :HEAD_DIM, at] = scaled.astype(jnp.bfloat16)
    high = lse.astype(jnp.bfloat16).astype(jnp.float32)
    mid = (lse - high).astype(jnp.bfloat16).astype(jnp.float32)
    low = lse - high - mid
    line = lax.broadcasted_iota(jnp.int32, (EXTRA, SUB), 0)
    lines = jnp.where(line == 0, high, jnp.where(line == 1, mid, low))
    out_ref[h, HEAD_DIM:, at] = lines.astype(jnp.bfloat16)


def write_kept(out_ref, lse_ref, h, at, scaled, lse):
    out_ref[h, :, at] = scaled
    lse_ref[h, :, at] = jnp.broadcast_to(lse, (8, SUB))


def ctx_of(place):
    return place[0] // HEADS_AXIS


def late_side(place):
    return jnp.where(ctx_of(place) < 2, 0, 1)


def early_side(place):
    return jnp.where(ctx_of(place) == 0, 1, 0)


def own_source(block, k_ref, v_ref):
    return block, lambda h, take: k_ref[take, cols_of(h)], lambda: v_ref[...]


def fetch(place, left_ref, right_ref, held, sem):
    left = ctx_of(place) < 2

    @pl.when(left)
    def _():
        copy = pltpu.make_async_copy(left_ref, held, sem)
        copy.start()
        copy.wait()

    @pl.when(jnp.logical_not(left))
    def _():
        copy = pltpu.make_async_copy(right_ref, held, sem)
        copy.start()
        copy.wait()


def got_source(block, held):
    return block, lambda h, take: held[0, take, cols_of(h)], lambda: held[1]


def own_kernel(place, bounds, q_ref, k_ref, v_ref, out_ref, lse_ref, *state):
    ctx = ctx_of(place)
    finish = functools.partial(write_kept, out_ref, lse_ref)
    fold_tiles(bounds, ctx, q_ref[...], [own_source(ctx, k_ref, v_ref)], SIDE, state, finish, SUB)


def early_kernel(place, bounds, q_ref, k_ref, v_ref, out_ref, *state):
    ctx = ctx_of(place)

    @pl.when((ctx == 0) | (ctx == 2))
    def _():
        finish = functools.partial(write_message, out_ref)
        fold_tiles(bounds, ctx + 1, q_ref[...], [own_source(ctx, k_ref, v_ref)], SIDE, state, finish)


def carry_kernel(place, bounds, ql_ref, qr_ref, k_ref, v_ref, out_ref, lse_ref, *state):
    ctx = ctx_of(place)

    @pl.when(ctx < 3)
    def _():
        query = jnp.where(ctx < 2, ql_ref[...], qr_ref[...])
        finish = functools.partial(write_kept, out_ref, lse_ref)
        fold_tiles(
            bounds, pick(ctx, 3, 2, 3, 2), query, [own_source(ctx, k_ref, v_ref)], SIDE, state, finish
        )


def late_kernel(
    place, bounds, ql_ref, qr_ref, part_ref, part_lse, q_ref, left_ref, right_ref, out_ref, got_ref, got_lse,
    held, sem, *state
):
    ctx = ctx_of(place)
    fetch(place, left_ref, right_ref, held, sem)
    query = jnp.where(ctx < 2, ql_ref[...], qr_ref[...])
    carried = ctx < 3
    source = got_source(pick(ctx, 1, 0, 1, 0), held)

    def finish(h, at, scaled, lse):
        other = jnp.where(carried, part_lse[h, 0:1, at], NEG_FILL)
        before = jnp.where(carried, part_ref[h, :, at], 0.0)
        peak = jnp.maximum(lse, other)
        here, there = jnp.exp2(lse - peak), jnp.exp2(other - peak)
        both = here + there
        write_message(out_ref, h, at, (scaled * here + before * there) / both, peak + jnp.log2(both))

    fold_tiles(bounds, pick(ctx, 3, 2, 3, 2), query, [source], SIDE, state, finish, turn=ctx >= 0)

    @pl.when(ctx >= 1)
    def _():
        keep = functools.partial(write_kept, got_ref, got_lse)
        fold_tiles(bounds, ctx, q_ref[...], [source], SIDE, state, keep, turn=ctx < 0)


def fold_call(kernel, name, work, rows, steps, in_specs, message, got, arrays, place, bounds):
    half = SIDE * HEAD_DIM
    out_shape, out_specs = (), ()
    if message:
        out_shape = (jax.ShapeDtypeStruct((steps * SIDE, HEAD_DIM + EXTRA, rows), jnp.bfloat16),)
        out_specs = (pl.BlockSpec((SIDE, HEAD_DIM + EXTRA, rows), lambda i, *_: (i, 0, 0)),)
    if got or not message:
        out_shape += (
            jax.ShapeDtypeStruct((steps * SIDE, HEAD_DIM, rows), jnp.float32),
            jax.ShapeDtypeStruct((steps * SIDE, 8, rows), jnp.float32),
        )
        out_specs += (
            pl.BlockSpec((SIDE, HEAD_DIM, rows), lambda i, *_: (i, 0, 0)),
            pl.BlockSpec((SIDE, 8, rows), lambda i, *_: (i, 0, 0)),
        )
    scratch = [pltpu.VMEM((2, rows, half), jnp.bfloat16), pltpu.SemaphoreType.DMA] if got else []
    scratch += [
        pltpu.VMEM((SIDE, 1, SUB), jnp.float32),
        pltpu.VMEM((SIDE, 1, SUB), jnp.float32),
        pltpu.VMEM((SIDE, HEAD_DIM, SUB), jnp.float32),
        pltpu.VMEM((half, rows), jnp.bfloat16),
        pltpu.VMEM((1, half, rows), jnp.bfloat16),
    ]
    return pl.pallas_call(
        kernel,
        out_shape=out_shape,
        grid_spec=pltpu.PrefetchScalarGridSpec(
            num_scalar_prefetch=2, grid=(steps,), in_specs=in_specs, out_specs=out_specs, scratch_shapes=scratch
        ),
        cost_estimate=pl.CostEstimate(flops=work, bytes_accessed=1, transcendentals=0),
        name=name,
    )(place, bounds, *arrays)


def pack_kernel(place, q_ref, k_ref, v_ref, left, right, q_l, q_r, q_x, held, in_sems, out_sems):
    half = SIDE * HEAD_DIM
    low, high = pl.ds(0, half), pl.ds(half, half)
    reads = [
        pltpu.make_async_copy(ref.at[:, cols], held.at[n], in_sems.at[n])
        for n, (ref, cols) in enumerate(
            [(k_ref, low), (v_ref, low), (k_ref, high), (v_ref, high), (q_ref, low), (q_ref, high)]
        )
    ]
    writes = [
        pltpu.make_async_copy(held.at[0:2], left, out_sems.at[0]),
        pltpu.make_async_copy(held.at[2:4], right, out_sems.at[1]),
        pltpu.make_async_copy(held.at[4], q_l, out_sems.at[2]),
        pltpu.make_async_copy(held.at[5], q_r, out_sems.at[3]),
        pltpu.make_async_copy(held.at[jnp.where(ctx_of(place) == 3, 4, 5)], q_x, out_sems.at[4]),
    ]
    for copy in reads:
        copy.start()
    for n, copy in enumerate(reads):
        copy.wait()
        for ready in {1: [0], 3: [1], 4: [2], 5: [3, 4]}.get(n, []):
            writes[ready].start()
    for copy in writes:
        copy.wait()


def pack(place, queries, keys, values):
    rows = keys.shape[0]
    half = SIDE * HEAD_DIM
    anywhere = pl.BlockSpec(memory_space=pl.ANY)
    both = jax.ShapeDtypeStruct((2, rows, half), jnp.bfloat16)
    single = jax.ShapeDtypeStruct((rows, half), jnp.bfloat16)
    return pl.pallas_call(
        pack_kernel,
        out_shape=(both, both, single, single, single),
        grid_spec=pltpu.PrefetchScalarGridSpec(
            num_scalar_prefetch=1,
            grid=(1,),
            in_specs=[anywhere] * 3,
            out_specs=[anywhere] * 5,
            scratch_shapes=[
                pltpu.VMEM((6, rows, half), jnp.bfloat16),
                pltpu.SemaphoreType.DMA((6,)),
                pltpu.SemaphoreType.DMA((5,)),
            ],
        ),
        name="pack",
    )(place, queries, keys, values)


def merge_kernel(place, own, own_lse, got, got_lse, one_ref, two_ref, three_ref, out_ref):
    ctx = ctx_of(place)

    def sent(ref, flag, h):
        tail = ref[h, HEAD_DIM:, :].astype(jnp.float32)
        lse = jnp.where(flag, tail[0:1, :] + tail[1:2, :] + tail[2:3, :], NEG_FILL)
        return jnp.where(flag, ref[h, :HEAD_DIM, :].astype(jnp.float32), 0.0), lse

    def kept(ref, lse_ref, flag, h):
        return jnp.where(flag, ref[h], 0.0), jnp.where(flag, lse_ref[h, 0:1, :], NEG_FILL)

    def combine(others):
        for h in range(SIDE):
            parts = [(own[h], own_lse[h, 0:1, :])] + others(h)
            peak = functools.reduce(jnp.maximum, [lse for _, lse in parts])
            shares = [jnp.exp2(lse - peak) for _, lse in parts]
            inverse = 1.0 / functools.reduce(jnp.add, shares)
            summed = functools.reduce(jnp.add, [out * (share * inverse) for (out, _), share in zip(parts, shares)])
            out_ref[:, cols_of(h)] = summed.astype(out_ref.dtype).T

    @pl.when(pl.program_id(0) == 0)
    def _():
        combine(
            lambda h: [kept(got, got_lse, ctx == 1, h), sent(one_ref, ctx >= 2, h), sent(three_ref, ctx == 3, h)]
        )

    @pl.when(pl.program_id(0) == 1)
    def _():
        combine(
            lambda h: [kept(got, got_lse, ctx >= 2, h), sent(two_ref, ctx >= 2, h), sent(three_ref, ctx == 1, h)]
        )


def merge(place, own, got, one, two, three):
    rows = one.shape[2]
    tall = HEAD_DIM + EXTRA
    moving = lambda i, *_: (i, 0, 0)
    fixed = lambda i, *_: (0, 0, 0)
    pair = lambda at: [pl.BlockSpec((SIDE, HEAD_DIM, rows), at), pl.BlockSpec((SIDE, 8, rows), at)]
    return pl.pallas_call(
        merge_kernel,
        out_shape=jax.ShapeDtypeStruct((rows, 2 * SIDE * HEAD_DIM), jnp.bfloat16),
        grid_spec=pltpu.PrefetchScalarGridSpec(
            num_scalar_prefetch=1,
            grid=(2,),
            in_specs=pair(moving) + pair(fixed) + [pl.BlockSpec((SIDE, tall, rows), fixed)] * 3,
            out_specs=pl.BlockSpec((rows, SIDE * HEAD_DIM), lambda i, *_: (0, i)),
        ),
        name="merge",
    )(place, *own, *got, one, two, three)


def on_device(mix_query, mix_key, mix_value, mr_filter, doc_ids, att_query, att_key, att_value):
    at_head = lax.axis_index("head")
    heads = lax.axis_size("head")
    blocks = lax.axis_size("ctx")
    half = SIDE * HEAD_DIM
    rows = att_key.shape[0]

    def pass_on(x, *pairs):
        return lax.ppermute(x, "ctx", list(pairs))

    place = jnp.reshape(lax.axis_index(("ctx", "head")), (1,)).astype(jnp.int32)
    pack_l, pack_r, query_l, query_r, query_x = pack(place, att_query, att_key, att_value)
    pack_l, pack_r, query_l, query_r, query_x, doc_ids, att_query, mix_key = lax.optimization_barrier(
        (pack_l, pack_r, query_l, query_r, query_x, doc_ids, att_query, mix_key)
    )
    kv_l = pass_on(pack_l, (0, 1), (1, 0))
    kv_r = pass_on(pack_r, (0, 3), (1, 2))
    q_x = pass_on(query_x, (3, 2), (1, 0))
    q_l = pass_on(query_l, (2, 1), (3, 0))
    q_r = pass_on(query_r, (2, 3), (3, 2))
    bounds = jnp.sum((doc_ids[None, :] < jnp.arange(4, dtype=jnp.int32)[:, None]).astype(jnp.int32), axis=1)

    product = (mix_key.astype(jnp.float32) * mix_value.astype(jnp.float32)).astype(jnp.bfloat16)
    width = product.shape[1]
    count = blocks * heads

    whole = pl.BlockSpec((rows, half), lambda i, *_: (0, 0))
    stepped = pl.BlockSpec((rows, half), lambda i, *_: (0, i))
    at_early = pl.BlockSpec((rows, half), lambda i, place, bounds: (0, early_side(place)))
    at_late = pl.BlockSpec((rows, half), lambda i, place, bounds: (0, late_side(place)))
    anywhere = pl.BlockSpec(memory_space=pl.ANY)
    part = [
        pl.BlockSpec((SIDE, HEAD_DIM, rows), lambda i, *_: (0, 0, 0)),
        pl.BlockSpec((SIDE, 8, rows), lambda i, *_: (0, 0, 0)),
    ]

    own = fold_call(
        own_kernel, "fold_own", 1, rows, 2, [stepped] * 3, False, False,
        (att_query, att_key, att_value), place, bounds,
    )
    own, q_x, q_l, q_r, product = lax.optimization_barrier((own, q_x, q_l, q_r, product))
    (early,) = fold_call(
        early_kernel, "fold_early", 1, rows, 1, [whole, at_early, at_early], True, False,
        (q_x, att_key, att_value), place, bounds,
    )
    part_3 = pass_on(early, (0, 1), (2, 3))
    q_l, q_r, early = lax.optimization_barrier((q_l, q_r, early))
    carry = fold_call(
        carry_kernel, "fold_carry", 1, rows, 1, [whole, whole, at_late, at_late], False, False,
        (q_l, q_r, att_key, att_value), place, bounds,
    )
    carry, kv_l, kv_r, product = lax.optimization_barrier((carry, kv_l, kv_r, product))
    prod_a, prod_b = product[:, : width // 2], product[:, width // 2 :]
    rim_a = lax.ppermute(prod_a, ("ctx", "head"), [(i, i + 1) for i in range(count - 1)])
    staged = lax.ppermute(
        prod_b, ("ctx", "head"), [(i, i + heads) for i in range(count - heads) if i % heads == heads - 1]
    )
    late, *got = fold_call(
        late_kernel, "fold_late", 1, rows, 1, [whole, whole, *part, at_late, anywhere, anywhere], True, True,
        (q_l, q_r, *carry, att_query, kv_l, kv_r), place, bounds,
    )
    part_1 = pass_on(late, (0, 3), (1, 2))
    part_2 = pass_on(late, (2, 3), (3, 2))
    staged, prod_b, late, got = lax.optimization_barrier((staged, prod_b, late, got))
    rim_b = lax.ppermute(
        jnp.where(at_head == heads - 1, staged, prod_b), "head", [(i, (i + 1) % heads) for i in range(heads)]
    )
    mixed = mixer(place, bounds, rim_a, rim_b, product, mix_query, mr_filter)
    place, mixed = lax.optimization_barrier((place, mixed))
    attended = merge(place, own, got, part_1, part_2, part_3)
    return (mixed, attended)


def solution(mesh):
    placed = (
        P(("dp", "ctx", "head"), None),
        P(("dp", "ctx", "head"), None),
        P(("dp", "ctx", "head"), None),
        P(),
        P("dp"),
        P(("dp", "ctx"), "head"),
        P(("dp", "ctx"), "head"),
        P(("dp", "ctx"), "head"),
    )
    return jax.shard_map(
        on_device,
        mesh=mesh,
        in_specs=placed,
        out_specs=(P(("dp", "ctx", "head"), None), P(("dp", "ctx"), "head")),
        check_vma=False,
    )
```

time: 102 us -> 93.3 us (0.915); the launches traced: 100 us -> 92.7 us
  starting transfers between devices: 29.7 us -> 23.3 us
  Pallas kernels: 37.2 us -> 42 us
  local copies, waits for them, and re-layouts: 5.12 us -> 2.01 us
  waiting for transfers between devices: 23.3 us -> 21 us
    ppermute x8, waiting for transfers between devices: 23.3 us -> 15 us  [pass_on(): return lax.ppermute(x, 'ctx', list(pairs))]
    pallas_call x5, Pallas kernels: 21.8 us -> 27.8 us  [the longest x4 24.7 us: fold_call(): pl.pallas_call(kernel, out_shape=out_shape, grid_spec=pltpu.PrefetchScala...]
    ppermute x1, waiting for transfers between devices: 0.01 us -> 5.99 us  [on_device(): lax.ppermute(jnp.where(at_head == heads - 1, staged, prod_b), 'head', [(i...]
    ppermute x8, starting transfers between devices: 22.8 us -> 18.6 us  [pass_on(): return lax.ppermute(x, 'ctx', list(pairs))]
    another operation x2 -> x0, local copies, waits for them, and re-layouts: 2.46 us -> none  [on_device(): pack_r = jnp.stack([att_key[:, half:], att_value[:, half:]])]
    ppermute x1, starting transfers between devices: 4.29 us -> 2.05 us  [on_device(): lax.ppermute(jnp.where(at_head == heads - 1, staged, prod_b), 'head', [(i...]
    convert_element_type x1, other arithmetic: 0.49 us -> 2.71 us  [on_device(): (mix_key.astype(jnp.float32) * mix_value.astype(jnp.float32)).astype(jnp....]
    another operation x1 -> x0, other arithmetic: 1.5 us -> none  [on_device(): pack_l = jnp.stack([att_key[:, :half], att_value[:, :half]])]
  transfers between devices with their start and end apart: 11 -> 11, of which waited for: 3 -> 4; matrix products, arithmetic and copies ran while one was open for 1% -> 4% of each run, Pallas kernels for 33% -> 38%
where the time goes in v2:
time: 93.3 us; the launch traced here: 92.7 us
  Pallas kernels  42 us (45%)
  starting transfers between devices  23.3 us (25%)
  waiting for transfers between devices  21 us (23%)
  other arithmetic  3.56 us (4%)
  local copies, waits for them, and re-layouts  2.01 us (2%)
    pallas_call x4, Pallas kernels, fold_call(): pl.pallas_call(kernel, out_shape=out_shape, grid_spec=pltpu.PrefetchScala...  24.7 us
    ppermute x8, starting transfers between devices, pass_on(): return lax.ppermute(x, 'ctx', list(pairs))  18.6 us
    ppermute x8, waiting for transfers between devices, pass_on(): return lax.ppermute(x, 'ctx', list(pairs))  15 us
    pallas_call x1, Pallas kernels, mixer(): pl.pallas_call(functools.partial(conv_kernel, group_size), out_shape=jax....  10.2 us
    ppermute x1, waiting for transfers between devices, on_device(): lax.ppermute(jnp.where(at_head == heads - 1, staged, prod_b), 'head', [(i...  5.99 us
    pallas_call x1, Pallas kernels, merge(): pl.pallas_call(merge_kernel, out_shape=jax.ShapeDtypeStruct((rows, 2 * SI...  4.03 us
    pallas_call x1, Pallas kernels, pack(): pl.pallas_call(pack_kernel, out_shape=(both, both, single, single, single...  3.15 us
    convert_element_type x1, other arithmetic, on_device(): (mix_key.astype(jnp.float32) * mix_value.astype(jnp.float32)).astype(jnp....  2.71 us
  transfers between devices with their start and end apart: 11, of which 4 were waited for; matrix products, arithmetic and copies ran while one was open for 4% of the time, Pallas kernels for 38%

profile of v2, /device:TPU:118, one launch (start us, length us, event | category | flops | bytes accessed | tf_op | source)
XLA Modules:
  0.0 92.7 jit_solution(14930640613912490920)
XLA Ops:
  0.6 3.1 %pack.1 = (bf16[2,512,512]{2,1,0:T(8,128)(2,1)}, bf16[2,512,512]{2,1,0:T(8,128)(2,1)}, bf16[512,512]{1,0:T(8,128)(2,1)}, bf16[512,512]{1,0:T(8,128)(2,1)}, bf16[512,512]{1,0:T(8,128)(2,1)}) custom-call(s32[1]{0:T(128)} %bitcast.place, bf16[512,1024]{1,0:T(8,128)(2,1)} %q_ref.3, bf16[512,1024]{1,0:T(8,128)(2,1)} %k_ref.7, bf16[512,1024]{1,0:T(8,128)(2,1)} %v_ref.7), custom_call_target="tpu_custom_call" | custom-call | tf_op jit(solution)/shard_map/pack/pallas_call | solution.py:323
  3.8 0.0 copy-start.6
  3.8 3.6 %collective-permute-start = (bf16[512,512]{1,0:T(8,128)(2,1)}, bf16[512,512]{1,0:T(8,128)(2,1)}, u32[]{:S(2)}, u32[]{:S(2)}) collective-permute-start(bf16[512,512]{1,0:T(8,128)(2,1)} %get-tuple-element.50), channel_id=1, source_target_pairs={{12,8},{4,0},{13,9},{5,1},{14,10},{6,2},{15,11},{7,3},{28,24},{20,... | collective-permute-start | bytes 1572872 | tf_op jit(solution)/shard_map/ppermute | solution.py:401
  7.4 1.3 %collective-permute-start.1 = (bf16[512,512]{1,0:T(8,128)(2,1)}, bf16[512,512]{1,0:T(8,128)(2,1)S(1)}, u32[]{:S(2)}, u32[]{:S(2)}) collective-permute-start(bf16[512,512]{1,0:T(8,128)(2,1)} %get-tuple-element.51), channel_id=1, source_target_pairs={{8,4},{12,0},{9,5},{13,1},{10,6},{14,2},{11,7},{15,3},{24,20},{28,... | collective-permute-start | bytes 1572872 | tf_op jit(solution)/shard_map/ppermute | solution.py:401
  8.7 3.6 %collective-permute-start.2 = (bf16[512,512]{1,0:T(8,128)(2,1)}, bf16[512,512]{1,0:T(8,128)(2,1)S(1)}, u32[]{:S(2)}, u32[]{:S(2)}) collective-permute-start(bf16[512,512]{1,0:T(8,128)(2,1)} %get-tuple-element.52), channel_id=1, source_target_pairs={{8,12},{12,8},{9,13},{13,9},{10,14},{14,10},{11,15},{15,11},{24,28... | collective-permute-start | bytes 1572872 | tf_op jit(solution)/shard_map/ppermute | solution.py:401
  12.3 1.7 %collective-permute-start.3 = (bf16[2,512,512]{2,1,0:T(8,128)(2,1)}, bf16[2,512,512]{2,1,0:T(8,128)(2,1)}, u32[]{:S(2)}, u32[]{:S(2)}) collective-permute-start(bf16[2,512,512]{2,1,0:T(8,128)(2,1)} %get-tuple-element.61), channel_id=1, source_target_pairs={{0,4},{4,0},{1,5},{5,1},{2,6},{6,2},{3,7},{7,3},{16,20},{20,16},{1... | collective-permute-start | bytes 3145736 | tf_op jit(solution)/shard_map/ppermute | solution.py:401
  14.0 1.3 %collective-permute-start.4 = (bf16[2,512,512]{2,1,0:T(8,128)(2,1)}, bf16[2,512,512]{2,1,0:T(8,128)(2,1)}, u32[]{:S(2)}, u32[]{:S(2)}) collective-permute-start(bf16[2,512,512]{2,1,0:T(8,128)(2,1)} %get-tuple-element.62), channel_id=1, source_target_pairs={{0,12},{4,8},{1,13},{5,9},{2,14},{6,10},{3,15},{7,11},{16,28},{20,... | collective-permute-start | bytes 3145736 | tf_op jit(solution)/shard_map/ppermute | solution.py:401
  15.2 2.7 %multiply_convert_fusion.prod_ref = bf16[128,8192]{1,0:T(8,128)(2,1)S(1)} fusion(bf16[128,8192]{1,0:T(8,128)(2,1)} %param.10, bf16[128,8192]{1,0:T(8,128)(2,1)} %param.9), kind=kLoop, calls=%fused_computation | loop fusion | flops 4194304 | bytes 6291456 | tf_op jit(solution)/shard_map/convert_element_type | solution.py:415
  18.0 0.0 copy-done.6
  18.0 0.0 copy-start
  18.0 0.7 convert_reduce_fusion.bounds
  18.7 8.2 %fold_own.1 = (f32[8,128,512]{2,1,0:T(8,128)}, f32[8,8,512]{2,1,0:T(8,128)}) custom-call(s32[1]{0:T(128)} %bitcast.place, s32[4]{0:T(128)} %convert_reduce_fusion.bounds, bf16[512,1024]{1,0:T(8,128)(2,1)} %q_ref.3, bf16[512,1024]{1,0:T(8,128)(2,1)} %k_ref.7, bf16[512,1024]{1,0:T(8,128)(2,1)} %v_ref.7), custom_call_target="tpu_custom_call" | custom-call | flops 1 | bytes 1 | tf_op jit(solution)/shard_map/fold_own/pallas_call | solution.py:280
  26.9 0.0 collective-permute-done.q_ref
  26.9 0.0 collective-permute-done.1.ql_ref
  26.9 0.0 copy-start.1
  26.9 2.3 %collective-permute-done.2.qr_ref = bf16[512,512]{1,0:T(8,128)(2,1)S(1)} collective-permute-done((bf16[512,512]{1,0:T(8,128)(2,1)}, bf16[512,512]{1,0:T(8,128)(2,1)S(1)}, u32[]{:S(2)}, u32[]{:S(2)}) %collective-permute-start.2) | collective-permute-done | bytes 524320 | tf_op jit(solution)/shard_map/ppermute | solution.py:401
  29.3 0.0 copy-start.2
  29.3 2.8 %fold_early.1 = bf16[4,144,512]{2,1,0:T(8,128)(2,1)} custom-call(s32[1]{0:T(128)} %bitcast.place, s32[4]{0:T(128)} %convert_reduce_fusion.bounds, bf16[512,512]{1,0:T(8,128)(2,1)} %collective-permute-done.q_ref, bf16[512,1024]{1,0:T(8,128)(2,1)} %k_ref.7, bf16[512,1024]{1,0:T(8,128)(2,1)} %v_ref.7), custom_call_target="tpu_custom_call" | custom-call | flops 1 | bytes 1 | tf_op jit(solution)/shard_map/fold_early/pallas_call | solution.py:280
  32.1 0.0 copy-done.1
  32.1 0.0 copy-done.2
  32.1 3.3 %fold_carry.1 = (f32[4,128,512]{2,1,0:T(8,128)}, f32[4,8,512]{2,1,0:T(8,128)}) custom-call(s32[1]{0:T(128)} %bitcast.place, s32[4]{0:T(128)} %convert_reduce_fusion.bounds, bf16[512,512]{1,0:T(8,128)(2,1)} %copy-done.1, bf16[512,512]{1,0:T(8,128)(2,1)} %copy-done.2, bf16[512,1024]{1,0:T(8,128)(2,1)} %k_ref.7, bf16[512,1024]{1,0:T(8,128)(2,1)} %v_ref.7), custom_call_target="tpu_custom_call" | custom-call | flops 1 | bytes 1 | tf_op jit(solution)/shard_map/fold_carry/pallas_call | solution.py:280
  35.4 0.0 collective-permute-done.3.left_ref
  35.4 6.1 %collective-permute-done.4.right_ref = bf16[2,512,512]{2,1,0:T(8,128)(2,1)} collective-permute-done((bf16[2,512,512]{2,1,0:T(8,128)(2,1)}, bf16[2,512,512]{2,1,0:T(8,128)(2,1)}, u32[]{:S(2)}, u32[]{:S(2)}) %collective-permute-start.4) | collective-permute-done | bytes 1048608 | tf_op jit(solution)/shard_map/ppermute | solution.py:401
  41.4 0.0 copy-done
  41.4 1.2 %fusion = (bf16[128,4096]{1,0:T(8,128)(2,1)S(1)}, bf16[128,4096]{1,0:T(8,128)(2,1)}) fusion(bf16[128,8192]{1,0:T(8,128)(2,1)S(1)} %multiply_convert_fusion.prod_ref), kind=kLoop, calls=%fused_computation.4 | loop fusion | bytes 4194304 | tf_op jit(solution)/shard_map/slice | solution.py:445
  42.6 0.7 collective-permute-start.6
  43.3 1.9 %collective-permute-start.5 = (bf16[128,4096]{1,0:T(8,128)(2,1)}, bf16[128,4096]{1,0:T(8,128)(2,1)}, u32[]{:S(2)}, u32[]{:S(2)}) collective-permute-start(bf16[128,4096]{1,0:T(8,128)(2,1)} %get-tuple-element.81), channel_id=1, source_target_pairs={{0,1},{1,2},{2,3},{3,4},{4,5},{5,6},{6,7},{7,8},{8,9},{9,10},{10,1... | collective-permute-start | bytes 3145736 | tf_op jit(solution)/shard_map/ppermute | solution.py:446
  45.2 10.4 %fold_late.1 = (bf16[4,144,512]{2,1,0:T(8,128)(2,1)}, f32[4,128,512]{2,1,0:T(8,128)}, f32[4,8,512]{2,1,0:T(8,128)}) custom-call(s32[1]{0:T(128)} %bitcast.place, s32[4]{0:T(128)} %convert_reduce_fusion.bounds, bf16[512,512]{1,0:T(8,128)(2,1)} %copy-done.1, bf16[512,512]{1,0:T(8,128)(2,1)} %copy-done.2, f32[4,128,512]{2,1,0:T(8,128)} %get-tuple-element.65.part_ref, ...), custom_call_target="tpu_custom_call" | custom-call | flops 1 | bytes 1 | tf_op jit(solution)/shard_map/fold_late/pallas_call | solution.py:280
  55.6 0.0 collective-permute-done.6
  55.6 0.1 broadcast_select_fusion
  55.8 2.1 %collective-permute-start.7 = (bf16[128,4096]{1,0:T(8,128)(2,1)S(1)}, bf16[128,4096]{1,0:T(8,128)(2,1)}, u32[]{:S(2)}, u32[]{:S(2)}) collective-permute-start(bf16[128,4096]{1,0:T(8,128)(2,1)S(1)} %broadcast_select_fusion), channel_id=1, source_target_pairs={{0,1},{1,2},{2,3},{3,0},{4,5},{5,6},{6,7},{7,4},{8,9},{9,10},{10,1... | collective-permute-start | bytes 3145736 | tf_op jit(solution)/shard_map/ppermute | solution.py:457
  57.8 1.3 %collective-permute-start.10 = (bf16[4,144,512]{2,1,0:T(8,128)(2,1)}, bf16[4,144,512]{2,1,0:T(8,128)(2,1)S(1)}, u32[]{:S(2)}, u32[]{:S(2)}) collective-permute-start(bf16[4,144,512]{2,1,0:T(8,128)(2,1)} %fold_early.1), channel_id=1, source_target_pairs={{0,4},{8,12},{1,5},{9,13},{2,6},{10,14},{3,7},{11,15},{16,20},{24,... | collective-permute-start | bytes 1769480 | tf_op jit(solution)/shard_map/ppermute | solution.py:401
  59.1 1.3 %collective-permute-start.8 = (bf16[4,144,512]{2,1,0:T(8,128)(2,1)}, bf16[4,144,512]{2,1,0:T(8,128)(2,1)S(1)}, u32[]{:S(2)}, u32[]{:S(2)}) collective-permute-start(bf16[4,144,512]{2,1,0:T(8,128)(2,1)} %get-tuple-element.69), channel_id=1, source_target_pairs={{0,12},{4,8},{1,13},{5,9},{2,14},{6,10},{3,15},{7,11},{16,28},{20,... | collective-permute-start | bytes 1769480 | tf_op jit(solution)/shard_map/ppermute | solution.py:401
  60.4 4.6 %collective-permute-start.9 = (bf16[4,144,512]{2,1,0:T(8,128)(2,1)}, bf16[4,144,512]{2,1,0:T(8,128)(2,1)S(1)}, u32[]{:S(2)}, u32[]{:S(2)}) collective-permute-start(bf16[4,144,512]{2,1,0:T(8,128)(2,1)} %get-tuple-element.69), channel_id=1, source_target_pairs={{8,12},{12,8},{9,13},{13,9},{10,14},{14,10},{11,15},{15,11},{24,28... | collective-permute-start | bytes 1769480 | tf_op jit(solution)/shard_map/ppermute | solution.py:401
  65.0 0.0 collective-permute-done.5.rim_a_ref
  65.0 6.0 %collective-permute-done.7.rim_b_ref = bf16[128,4096]{1,0:T(8,128)(2,1)} collective-permute-done((bf16[128,4096]{1,0:T(8,128)(2,1)S(1)}, bf16[128,4096]{1,0:T(8,128)(2,1)}, u32[]{:S(2)}, u32[]{:S(2)}) %collective-permute-start.7) | collective-permute-done | bytes 1048608 | tf_op jit(solution)/shard_map/ppermute | solution.py:457
  71.0 10.2 %mixer.1 = bf16[128,8192]{1,0:T(8,128)(2,1)} custom-call(s32[1]{0:T(128)} %bitcast.place, s32[4]{0:T(128)} %convert_reduce_fusion.bounds, bf16[128,4096]{1,0:T(8,128)(2,1)} %collective-permute-done.5.rim_a_ref, bf16[128,4096]{1,0:T(8,128)(2,1)} %collective-permute-done.7.rim_b_ref, bf16[128,8192]{1,0:T(8,128)(2,1)} %copy-done, bf16[128,8192]{1,0:T(8,128)(2,1)} %query_ref.1, ...), custom_call_target="tpu_custom_call" | custom-call | flops 8589934592 | bytes 8388608 | tf_op jit(solution)/shard_map/mixer/pallas_call | solution.py:68
  81.2 0.0 collective-permute-done.10.three_ref
  81.2 0.0 copy-start.3
  81.2 0.0 collective-permute-done.8.one_ref
  81.2 0.0 copy-start.4
  81.2 6.6 %collective-permute-done.9.two_ref = bf16[4,144,512]{2,1,0:T(8,128)(2,1)S(1)} collective-permute-done((bf16[4,144,512]{2,1,0:T(8,128)(2,1)}, bf16[4,144,512]{2,1,0:T(8,128)(2,1)S(1)}, u32[]{:S(2)}, u32[]{:S(2)}) %collective-permute-start.9) | collective-permute-done | bytes 589856 | tf_op jit(solution)/shard_map/ppermute | solution.py:401
  87.8 0.0 copy-done.3
  87.8 0.0 copy-done.4
  87.8 0.0 copy-start.5
  87.8 0.8 copy-done.5
  88.6 4.0 %merge.1 = bf16[512,1024]{1,0:T(8,128)(2,1)} custom-call(s32[1]{0:T(128)} %bitcast.place, f32[8,128,512]{2,1,0:T(8,128)} %get-tuple-element.76.own, f32[8,8,512]{2,1,0:T(8,128)} %get-tuple-element.77.own_lse, f32[4,128,512]{2,1,0:T(8,128)} %get-tuple-element.78.got, f32[4,8,512]{2,1,0:T(8,128)} %get-tuple-element.79.got_lse, bf16[4,144,512]{2,1,0:T(8,128)(2,1)} %copy-done.4, ...), custom_call_target="tpu_custom_call" | custom-call | tf_op jit(solution)/shard_map/merge/pallas_call | solution.py:380
Async XLA Ops:
  3.8 14.2 %copy-start.6 = (s32[2048]{0:T(1024)S(1)}, s32[2048]{0:T(1024)}, u32[]{:S(2)}) copy-start(s32[2048]{0:T(1024)} %param.12) | copy-start | bytes 24580
  3.8 23.1 %collective-permute-start = (bf16[512,512]{1,0:T(8,128)(2,1)}, bf16[512,512]{1,0:T(8,128)(2,1)}, u32[]{:S(2)}, u32[]{:S(2)}) collective-permute-start(bf16[512,512]{1,0:T(8,128)(2,1)} %get-tuple-element.50), channel_id=1, source_target_pairs={{12,8},{4,0},{13,9},{5,1},{14,10},{6,2},{15,11},{7,3},{28,24},{20,... | collective-permute-start | bytes 1572872 | tf_op jit(solution)/shard_map/ppermute | solution.py:401
  7.4 19.6 %collective-permute-start.1 = (bf16[512,512]{1,0:T(8,128)(2,1)}, bf16[512,512]{1,0:T(8,128)(2,1)S(1)}, u32[]{:S(2)}, u32[]{:S(2)}) collective-permute-start(bf16[512,512]{1,0:T(8,128)(2,1)} %get-tuple-element.51), channel_id=1, source_target_pairs={{8,4},{12,0},{9,5},{13,1},{10,6},{14,2},{11,7},{15,3},{24,20},{28,... | collective-permute-start | bytes 1572872 | tf_op jit(solution)/shard_map/ppermute | solution.py:401
  8.7 20.6 %collective-permute-start.2 = (bf16[512,512]{1,0:T(8,128)(2,1)}, bf16[512,512]{1,0:T(8,128)(2,1)S(1)}, u32[]{:S(2)}, u32[]{:S(2)}) collective-permute-start(bf16[512,512]{1,0:T(8,128)(2,1)} %get-tuple-element.52), channel_id=1, source_target_pairs={{8,12},{12,8},{9,13},{13,9},{10,14},{14,10},{11,15},{15,11},{24,28... | collective-permute-start | bytes 1572872 | tf_op jit(solution)/shard_map/ppermute | solution.py:401
  12.3 23.1 %collective-permute-start.3 = (bf16[2,512,512]{2,1,0:T(8,128)(2,1)}, bf16[2,512,512]{2,1,0:T(8,128)(2,1)}, u32[]{:S(2)}, u32[]{:S(2)}) collective-permute-start(bf16[2,512,512]{2,1,0:T(8,128)(2,1)} %get-tuple-element.61), channel_id=1, source_target_pairs={{0,4},{4,0},{1,5},{5,1},{2,6},{6,2},{3,7},{7,3},{16,20},{20,16},{1... | collective-permute-start | bytes 3145736 | tf_op jit(solution)/shard_map/ppermute | solution.py:401
  14.0 27.5 %collective-permute-start.4 = (bf16[2,512,512]{2,1,0:T(8,128)(2,1)}, bf16[2,512,512]{2,1,0:T(8,128)(2,1)}, u32[]{:S(2)}, u32[]{:S(2)}) collective-permute-start(bf16[2,512,512]{2,1,0:T(8,128)(2,1)} %get-tuple-element.62), channel_id=1, source_target_pairs={{0,12},{4,8},{1,13},{5,9},{2,14},{6,10},{3,15},{7,11},{16,28},{20,... | collective-permute-start | bytes 3145736 | tf_op jit(solution)/shard_map/ppermute | solution.py:401
  18.0 23.5 %copy-start = (bf16[128,8192]{1,0:T(8,128)(2,1)}, bf16[128,8192]{1,0:T(8,128)(2,1)S(1)}, u32[]{:S(2)}) copy-start(bf16[128,8192]{1,0:T(8,128)(2,1)S(1)} %multiply_convert_fusion.prod_ref) | copy-start | bytes 6291460
  26.9 5.2 %copy-start.1 = (bf16[512,512]{1,0:T(8,128)(2,1)}, bf16[512,512]{1,0:T(8,128)(2,1)S(1)}, u32[]{:S(2)}) copy-start(bf16[512,512]{1,0:T(8,128)(2,1)S(1)} %collective-permute-done.1.ql_ref) | copy-start | bytes 1572868
  29.3 2.8 %copy-start.2 = (bf16[512,512]{1,0:T(8,128)(2,1)}, bf16[512,512]{1,0:T(8,128)(2,1)S(1)}, u32[]{:S(2)}) copy-start(bf16[512,512]{1,0:T(8,128)(2,1)S(1)} %collective-permute-done.2.qr_ref) | copy-start | bytes 1572868
  42.6 13.0 %collective-permute-start.6 = (bf16[128,4096]{1,0:T(8,128)(2,1)S(1)}, bf16[128,4096]{1,0:T(8,128)(2,1)S(1)}, u32[]{:S(2)}, u32[]{:S(2)}) collective-permute-start(bf16[128,4096]{1,0:T(8,128)(2,1)S(1)} %get-tuple-element.73), channel_id=1, source_target_pairs={{3,7},{7,11},{11,15},{19,23},{23,27},{27,31},{35,39},{39,43},{43,4... | collective-permute-start | bytes 3145736 | tf_op jit(solution)/shard_map/ppermute | solution.py:447
  43.3 21.7 %collective-permute-start.5 = (bf16[128,4096]{1,0:T(8,128)(2,1)}, bf16[128,4096]{1,0:T(8,128)(2,1)}, u32[]{:S(2)}, u32[]{:S(2)}) collective-permute-start(bf16[128,4096]{1,0:T(8,128)(2,1)} %get-tuple-element.81), channel_id=1, source_target_pairs={{0,1},{1,2},{2,3},{3,4},{4,5},{5,6},{6,7},{7,8},{8,9},{9,10},{10,1... | collective-permute-start | bytes 3145736 | tf_op jit(solution)/shard_map/ppermute | solution.py:446
  55.8 15.2 %collective-permute-start.7 = (bf16[128,4096]{1,0:T(8,128)(2,1)S(1)}, bf16[128,4096]{1,0:T(8,128)(2,1)}, u32[]{:S(2)}, u32[]{:S(2)}) collective-permute-start(bf16[128,4096]{1,0:T(8,128)(2,1)S(1)} %broadcast_select_fusion), channel_id=1, source_target_pairs={{0,1},{1,2},{2,3},{3,0},{4,5},{5,6},{6,7},{7,4},{8,9},{9,10},{10,1... | collective-permute-start | bytes 3145736 | tf_op jit(solution)/shard_map/ppermute | solution.py:457
  57.8 23.4 %collective-permute-start.10 = (bf16[4,144,512]{2,1,0:T(8,128)(2,1)}, bf16[4,144,512]{2,1,0:T(8,128)(2,1)S(1)}, u32[]{:S(2)}, u32[]{:S(2)}) collective-permute-start(bf16[4,144,512]{2,1,0:T(8,128)(2,1)} %fold_early.1), channel_id=1, source_target_pairs={{0,4},{8,12},{1,5},{9,13},{2,6},{10,14},{3,7},{11,15},{16,20},{24,... | collective-permute-start | bytes 1769480 | tf_op jit(solution)/shard_map/ppermute | solution.py:401
  59.1 22.1 %collective-permute-start.8 = (bf16[4,144,512]{2,1,0:T(8,128)(2,1)}, bf16[4,144,512]{2,1,0:T(8,128)(2,1)S(1)}, u32[]{:S(2)}, u32[]{:S(2)}) collective-permute-start(bf16[4,144,512]{2,1,0:T(8,128)(2,1)} %get-tuple-element.69), channel_id=1, source_target_pairs={{0,12},{4,8},{1,13},{5,9},{2,14},{6,10},{3,15},{7,11},{16,28},{20,... | collective-permute-start | bytes 1769480 | tf_op jit(solution)/shard_map/ppermute | solution.py:401
  60.4 27.4 %collective-permute-start.9 = (bf16[4,144,512]{2,1,0:T(8,128)(2,1)}, bf16[4,144,512]{2,1,0:T(8,128)(2,1)S(1)}, u32[]{:S(2)}, u32[]{:S(2)}) collective-permute-start(bf16[4,144,512]{2,1,0:T(8,128)(2,1)} %get-tuple-element.69), channel_id=1, source_target_pairs={{8,12},{12,8},{9,13},{13,9},{10,14},{14,10},{11,15},{15,11},{24,28... | collective-permute-start | bytes 1769480 | tf_op jit(solution)/shard_map/ppermute | solution.py:401
  81.2 6.6 %copy-start.3 = (bf16[4,144,512]{2,1,0:T(8,128)(2,1)}, bf16[4,144,512]{2,1,0:T(8,128)(2,1)S(1)}, u32[]{:S(2)}) copy-start(bf16[4,144,512]{2,1,0:T(8,128)(2,1)S(1)} %collective-permute-done.10.three_ref) | copy-start | bytes 1769476
  81.2 6.6 %copy-start.4 = (bf16[4,144,512]{2,1,0:T(8,128)(2,1)}, bf16[4,144,512]{2,1,0:T(8,128)(2,1)S(1)}, u32[]{:S(2)}) copy-start(bf16[4,144,512]{2,1,0:T(8,128)(2,1)S(1)} %collective-permute-done.8.one_ref) | copy-start | bytes 1769476
  87.8 0.8 copy-start.5

commit v3 on v2

--- a/solution.py
+++ b/solution.py
@@ -13,7 +13,7 @@
 LOG2_SCALE = math.log2(math.e) / math.sqrt(HEAD_DIM)
 SIDE = 4
 SUB = 256
-EXTRA = 16
+EXTRA = 8
 COLS = 2048
 HEADS_AXIS = 4
 

time: 93.3 us -> 91.8 us (0.984)
  starting transfers between devices: 23.3 us -> 27.6 us
  Pallas kernels: 42 us -> 37.7 us
  waiting for transfers between devices: 21 us -> 19.5 us
    pallas_call x4, Pallas kernels: 24.7 us -> 20.3 us  [fold_call(): pl.pallas_call(kernel, out_shape=out_shape, grid_spec=pltpu.PrefetchScala...]
    ppermute x1, starting transfers between devices: 2.05 us -> 6.35 us  [on_device(): lax.ppermute(jnp.where(at_head == heads - 1, staged, prod_b), 'head', [(i...]
    ppermute x8, waiting for transfers between devices: 15 us -> 13.5 us  [pass_on(): return lax.ppermute(x, 'ctx', list(pairs))]
  transfers between devices with their start and end apart: 11 -> 11, of which waited for: 4 -> 4; matrix products, arithmetic and copies ran while one was open for 4% -> 4% of each run, Pallas kernels for 38% -> 33%
where the time goes in v3:
time: 91.8 us; the launch traced here: 91.2 us
  Pallas kernels  37.7 us (41%)
  starting transfers between devices  27.6 us (30%)
  waiting for transfers between devices  19.5 us (21%)
  other arithmetic  3.68 us (4%)
  local copies, waits for them, and re-layouts  1.99 us (2%)
    pallas_call x4, Pallas kernels, fold_call(): pl.pallas_call(kernel, out_shape=out_shape, grid_spec=pltpu.PrefetchScala...  20.3 us
    ppermute x8, starting transfers between devices, pass_on(): return lax.ppermute(x, 'ctx', list(pairs))  18.6 us
    ppermute x8, waiting for transfers between devices, pass_on(): return lax.ppermute(x, 'ctx', list(pairs))  13.5 us
    pallas_call x1, Pallas kernels, mixer(): pl.pallas_call(functools.partial(conv_kernel, group_size), out_shape=jax....  10.2 us
    ppermute x1, starting transfers between devices, on_device(): lax.ppermute(jnp.where(at_head == heads - 1, staged, prod_b), 'head', [(i...  6.35 us
    ppermute x1, waiting for transfers between devices, on_device(): lax.ppermute(jnp.where(at_head == heads - 1, staged, prod_b), 'head', [(i...  5.99 us
    pallas_call x1, Pallas kernels, merge(): pl.pallas_call(merge_kernel, out_shape=jax.ShapeDtypeStruct((rows, 2 * SI...  4 us
    pallas_call x1, Pallas kernels, pack(): pl.pallas_call(pack_kernel, out_shape=(both, both, single, single, single...  3.15 us
  transfers between devices with their start and end apart: 11, of which 4 were waited for; matrix products, arithmetic and copies ran while one was open for 4% of the time, Pallas kernels for 33%

profile of v3, /device:TPU:118, one launch (start us, length us, event | category | flops | bytes accessed | tf_op | source)
XLA Modules:
  0.0 91.2 jit_solution(15904833323155820343)
XLA Ops:
  0.6 3.1 %pack.1 = (bf16[2,512,512]{2,1,0:T(8,128)(2,1)}, bf16[2,512,512]{2,1,0:T(8,128)(2,1)}, bf16[512,512]{1,0:T(8,128)(2,1)}, bf16[512,512]{1,0:T(8,128)(2,1)}, bf16[512,512]{1,0:T(8,128)(2,1)}) custom-call(s32[1]{0:T(128)} %bitcast.place, bf16[512,1024]{1,0:T(8,128)(2,1)} %q_ref.3, bf16[512,1024]{1,0:T(8,128)(2,1)} %k_ref.7, bf16[512,1024]{1,0:T(8,128)(2,1)} %v_ref.7), custom_call_target="tpu_custom_call" | custom-call | tf_op jit(solution)/shard_map/pack/pallas_call | solution.py:323
  3.8 0.0 copy-start.6
  3.8 3.6 %collective-permute-start = (bf16[512,512]{1,0:T(8,128)(2,1)}, bf16[512,512]{1,0:T(8,128)(2,1)}, u32[]{:S(2)}, u32[]{:S(2)}) collective-permute-start(bf16[512,512]{1,0:T(8,128)(2,1)} %get-tuple-element.50), channel_id=1, source_target_pairs={{12,8},{4,0},{13,9},{5,1},{14,10},{6,2},{15,11},{7,3},{28,24},{20,... | collective-permute-start | bytes 1572872 | tf_op jit(solution)/shard_map/ppermute | solution.py:401
  7.4 1.3 %collective-permute-start.1 = (bf16[512,512]{1,0:T(8,128)(2,1)}, bf16[512,512]{1,0:T(8,128)(2,1)S(1)}, u32[]{:S(2)}, u32[]{:S(2)}) collective-permute-start(bf16[512,512]{1,0:T(8,128)(2,1)} %get-tuple-element.51), channel_id=1, source_target_pairs={{8,4},{12,0},{9,5},{13,1},{10,6},{14,2},{11,7},{15,3},{24,20},{28,... | collective-permute-start | bytes 1572872 | tf_op jit(solution)/shard_map/ppermute | solution.py:401
  8.7 3.6 %collective-permute-start.2 = (bf16[512,512]{1,0:T(8,128)(2,1)}, bf16[512,512]{1,0:T(8,128)(2,1)S(1)}, u32[]{:S(2)}, u32[]{:S(2)}) collective-permute-start(bf16[512,512]{1,0:T(8,128)(2,1)} %get-tuple-element.52), channel_id=1, source_target_pairs={{8,12},{12,8},{9,13},{13,9},{10,14},{14,10},{11,15},{15,11},{24,28... | collective-permute-start | bytes 1572872 | tf_op jit(solution)/shard_map/ppermute | solution.py:401
  12.3 1.7 %collective-permute-start.3 = (bf16[2,512,512]{2,1,0:T(8,128)(2,1)}, bf16[2,512,512]{2,1,0:T(8,128)(2,1)}, u32[]{:S(2)}, u32[]{:S(2)}) collective-permute-start(bf16[2,512,512]{2,1,0:T(8,128)(2,1)} %get-tuple-element.61), channel_id=1, source_target_pairs={{0,4},{4,0},{1,5},{5,1},{2,6},{6,2},{3,7},{7,3},{16,20},{20,16},{1... | collective-permute-start | bytes 3145736 | tf_op jit(solution)/shard_map/ppermute | solution.py:401
  14.0 1.3 %collective-permute-start.4 = (bf16[2,512,512]{2,1,0:T(8,128)(2,1)}, bf16[2,512,512]{2,1,0:T(8,128)(2,1)}, u32[]{:S(2)}, u32[]{:S(2)}) collective-permute-start(bf16[2,512,512]{2,1,0:T(8,128)(2,1)} %get-tuple-element.62), channel_id=1, source_target_pairs={{0,12},{4,8},{1,13},{5,9},{2,14},{6,10},{3,15},{7,11},{16,28},{20,... | collective-permute-start | bytes 3145736 | tf_op jit(solution)/shard_map/ppermute | solution.py:401
  15.3 2.7 %multiply_convert_fusion.prod_ref = bf16[128,8192]{1,0:T(8,128)(2,1)S(1)} fusion(bf16[128,8192]{1,0:T(8,128)(2,1)} %param.10, bf16[128,8192]{1,0:T(8,128)(2,1)} %param.9), kind=kLoop, calls=%fused_computation | loop fusion | flops 4194304 | bytes 6291456 | tf_op jit(solution)/shard_map/convert_element_type | solution.py:415
  18.0 0.0 copy-done.6
  18.0 0.0 copy-start
  18.0 0.8 convert_reduce_fusion.bounds
  18.9 8.2 %fold_own.1 = (f32[8,128,512]{2,1,0:T(8,128)}, f32[8,8,512]{2,1,0:T(8,128)}) custom-call(s32[1]{0:T(128)} %bitcast.place, s32[4]{0:T(128)} %convert_reduce_fusion.bounds, bf16[512,1024]{1,0:T(8,128)(2,1)} %q_ref.3, bf16[512,1024]{1,0:T(8,128)(2,1)} %k_ref.7, bf16[512,1024]{1,0:T(8,128)(2,1)} %v_ref.7), custom_call_target="tpu_custom_call" | custom-call | flops 1 | bytes 1 | tf_op jit(solution)/shard_map/fold_own/pallas_call | solution.py:280
  27.0 0.0 collective-permute-done.q_ref
  27.0 0.0 collective-permute-done.1.ql_ref
  27.0 0.0 copy-start.1
  27.0 2.2 %collective-permute-done.2.qr_ref = bf16[512,512]{1,0:T(8,128)(2,1)S(1)} collective-permute-done((bf16[512,512]{1,0:T(8,128)(2,1)}, bf16[512,512]{1,0:T(8,128)(2,1)S(1)}, u32[]{:S(2)}, u32[]{:S(2)}) %collective-permute-start.2) | collective-permute-done | bytes 524320 | tf_op jit(solution)/shard_map/ppermute | solution.py:401
  29.3 0.0 copy-start.2
  29.3 2.8 %fold_early.1 = bf16[4,136,512]{2,1,0:T(8,128)(2,1)} custom-call(s32[1]{0:T(128)} %bitcast.place, s32[4]{0:T(128)} %convert_reduce_fusion.bounds, bf16[512,512]{1,0:T(8,128)(2,1)} %collective-permute-done.q_ref, bf16[512,1024]{1,0:T(8,128)(2,1)} %k_ref.7, bf16[512,1024]{1,0:T(8,128)(2,1)} %v_ref.7), custom_call_target="tpu_custom_call" | custom-call | flops 1 | bytes 1 | tf_op jit(solution)/shard_map/fold_early/pallas_call | solution.py:280
  32.1 0.0 copy-done.1
  32.1 0.0 copy-done.2
  32.1 3.3 %fold_carry.1 = (f32[4,128,512]{2,1,0:T(8,128)}, f32[4,8,512]{2,1,0:T(8,128)}) custom-call(s32[1]{0:T(128)} %bitcast.place, s32[4]{0:T(128)} %convert_reduce_fusion.bounds, bf16[512,512]{1,0:T(8,128)(2,1)} %copy-done.1, bf16[512,512]{1,0:T(8,128)(2,1)} %copy-done.2, bf16[512,1024]{1,0:T(8,128)(2,1)} %k_ref.7, bf16[512,1024]{1,0:T(8,128)(2,1)} %v_ref.7), custom_call_target="tpu_custom_call" | custom-call | flops 1 | bytes 1 | tf_op jit(solution)/shard_map/fold_carry/pallas_call | solution.py:280
  35.4 0.0 collective-permute-done.3.left_ref
  35.4 6.1 %collective-permute-done.4.right_ref = bf16[2,512,512]{2,1,0:T(8,128)(2,1)} collective-permute-done((bf16[2,512,512]{2,1,0:T(8,128)(2,1)}, bf16[2,512,512]{2,1,0:T(8,128)(2,1)}, u32[]{:S(2)}, u32[]{:S(2)}) %collective-permute-start.4) | collective-permute-done | bytes 1048608 | tf_op jit(solution)/shard_map/ppermute | solution.py:401
  41.4 0.0 copy-done
  41.4 1.2 %fusion = (bf16[128,4096]{1,0:T(8,128)(2,1)S(1)}, bf16[128,4096]{1,0:T(8,128)(2,1)}) fusion(bf16[128,8192]{1,0:T(8,128)(2,1)S(1)} %multiply_convert_fusion.prod_ref), kind=kLoop, calls=%fused_computation.4 | loop fusion | bytes 4194304 | tf_op jit(solution)/shard_map/slice | solution.py:445
  42.6 0.7 collective-permute-start.6
  43.3 1.9 %collective-permute-start.5 = (bf16[128,4096]{1,0:T(8,128)(2,1)}, bf16[128,4096]{1,0:T(8,128)(2,1)}, u32[]{:S(2)}, u32[]{:S(2)}) collective-permute-start(bf16[128,4096]{1,0:T(8,128)(2,1)} %get-tuple-element.81), channel_id=1, source_target_pairs={{0,1},{1,2},{2,3},{3,4},{4,5},{5,6},{6,7},{7,8},{8,9},{9,10},{10,1... | collective-permute-start | bytes 3145736 | tf_op jit(solution)/shard_map/ppermute | solution.py:446
  45.3 6.1 %fold_late.1 = (bf16[4,136,512]{2,1,0:T(8,128)(2,1)}, f32[4,128,512]{2,1,0:T(8,128)}, f32[4,8,512]{2,1,0:T(8,128)}) custom-call(s32[1]{0:T(128)} %bitcast.place, s32[4]{0:T(128)} %convert_reduce_fusion.bounds, bf16[512,512]{1,0:T(8,128)(2,1)} %copy-done.1, bf16[512,512]{1,0:T(8,128)(2,1)} %copy-done.2, f32[4,128,512]{2,1,0:T(8,128)} %get-tuple-element.65.part_ref, ...), custom_call_target="tpu_custom_call" | custom-call | flops 1 | bytes 1 | tf_op jit(solution)/shard_map/fold_late/pallas_call | solution.py:280
  51.3 0.0 collective-permute-done.6
  51.3 0.1 broadcast_select_fusion
  51.5 6.4 %collective-permute-start.7 = (bf16[128,4096]{1,0:T(8,128)(2,1)S(1)}, bf16[128,4096]{1,0:T(8,128)(2,1)}, u32[]{:S(2)}, u32[]{:S(2)}) collective-permute-start(bf16[128,4096]{1,0:T(8,128)(2,1)S(1)} %broadcast_select_fusion), channel_id=1, source_target_pairs={{0,1},{1,2},{2,3},{3,0},{4,5},{5,6},{6,7},{7,4},{8,9},{9,10},{10,1... | collective-permute-start | bytes 3145736 | tf_op jit(solution)/shard_map/ppermute | solution.py:457
  57.8 1.3 %collective-permute-start.10 = (bf16[4,136,512]{2,1,0:T(8,128)(2,1)}, bf16[4,136,512]{2,1,0:T(8,128)(2,1)S(1)}, u32[]{:S(2)}, u32[]{:S(2)}) collective-permute-start(bf16[4,136,512]{2,1,0:T(8,128)(2,1)} %fold_early.1), channel_id=1, source_target_pairs={{0,4},{8,12},{1,5},{9,13},{2,6},{10,14},{3,7},{11,15},{16,20},{24,... | collective-permute-start | bytes 1671176 | tf_op jit(solution)/shard_map/ppermute | solution.py:401
  59.1 1.3 %collective-permute-start.8 = (bf16[4,136,512]{2,1,0:T(8,128)(2,1)}, bf16[4,136,512]{2,1,0:T(8,128)(2,1)S(1)}, u32[]{:S(2)}, u32[]{:S(2)}) collective-permute-start(bf16[4,136,512]{2,1,0:T(8,128)(2,1)} %get-tuple-element.69), channel_id=1, source_target_pairs={{0,12},{4,8},{1,13},{5,9},{2,14},{6,10},{3,15},{7,11},{16,28},{20,... | collective-permute-start | bytes 1671176 | tf_op jit(solution)/shard_map/ppermute | solution.py:401
  60.4 4.6 %collective-permute-start.9 = (bf16[4,136,512]{2,1,0:T(8,128)(2,1)}, bf16[4,136,512]{2,1,0:T(8,128)(2,1)S(1)}, u32[]{:S(2)}, u32[]{:S(2)}) collective-permute-start(bf16[4,136,512]{2,1,0:T(8,128)(2,1)} %get-tuple-element.69), channel_id=1, source_target_pairs={{8,12},{12,8},{9,13},{13,9},{10,14},{14,10},{11,15},{15,11},{24,28... | collective-permute-start | bytes 1671176 | tf_op jit(solution)/shard_map/ppermute | solution.py:401
  65.0 0.0 collective-permute-done.5.rim_a_ref
  65.0 6.0 %collective-permute-done.7.rim_b_ref = bf16[128,4096]{1,0:T(8,128)(2,1)} collective-permute-done((bf16[128,4096]{1,0:T(8,128)(2,1)S(1)}, bf16[128,4096]{1,0:T(8,128)(2,1)}, u32[]{:S(2)}, u32[]{:S(2)}) %collective-permute-start.7) | collective-permute-done | bytes 1048608 | tf_op jit(solution)/shard_map/ppermute | solution.py:457
  71.0 10.2 %mixer.1 = bf16[128,8192]{1,0:T(8,128)(2,1)} custom-call(s32[1]{0:T(128)} %bitcast.place, s32[4]{0:T(128)} %convert_reduce_fusion.bounds, bf16[128,4096]{1,0:T(8,128)(2,1)} %collective-permute-done.5.rim_a_ref, bf16[128,4096]{1,0:T(8,128)(2,1)} %collective-permute-done.7.rim_b_ref, bf16[128,8192]{1,0:T(8,128)(2,1)} %copy-done, bf16[128,8192]{1,0:T(8,128)(2,1)} %query_ref.1, ...), custom_call_target="tpu_custom_call" | custom-call | flops 8589934592 | bytes 8388608 | tf_op jit(solution)/shard_map/mixer/pallas_call | solution.py:68
  81.2 0.0 collective-permute-done.10.three_ref
  81.2 0.0 copy-start.3
  81.2 0.0 collective-permute-done.8.one_ref
  81.2 0.0 copy-start.4
  81.2 5.2 %collective-permute-done.9.two_ref = bf16[4,136,512]{2,1,0:T(8,128)(2,1)S(1)} collective-permute-done((bf16[4,136,512]{2,1,0:T(8,128)(2,1)}, bf16[4,136,512]{2,1,0:T(8,128)(2,1)S(1)}, u32[]{:S(2)}, u32[]{:S(2)}) %collective-permute-start.9) | collective-permute-done | bytes 557088 | tf_op jit(solution)/shard_map/ppermute | solution.py:401
  86.4 0.0 copy-done.3
  86.4 0.0 copy-done.4
  86.4 0.0 copy-start.5
  86.4 0.8 copy-done.5
  87.2 4.0 %merge.1 = bf16[512,1024]{1,0:T(8,128)(2,1)} custom-call(s32[1]{0:T(128)} %bitcast.place, f32[8,128,512]{2,1,0:T(8,128)} %get-tuple-element.76.own, f32[8,8,512]{2,1,0:T(8,128)} %get-tuple-element.77.own_lse, f32[4,128,512]{2,1,0:T(8,128)} %get-tuple-element.78.got, f32[4,8,512]{2,1,0:T(8,128)} %get-tuple-element.79.got_lse, bf16[4,136,512]{2,1,0:T(8,128)(2,1)} %copy-done.4, ...), custom_call_target="tpu_custom_call" | custom-call | tf_op jit(solution)/shard_map/merge/pallas_call | solution.py:380
Async XLA Ops:
  3.8 14.2 %copy-start.6 = (s32[2048]{0:T(1024)S(1)}, s32[2048]{0:T(1024)}, u32[]{:S(2)}) copy-start(s32[2048]{0:T(1024)} %param.12) | copy-start | bytes 24580
  3.8 23.2 %collective-permute-start = (bf16[512,512]{1,0:T(8,128)(2,1)}, bf16[512,512]{1,0:T(8,128)(2,1)}, u32[]{:S(2)}, u32[]{:S(2)}) collective-permute-start(bf16[512,512]{1,0:T(8,128)(2,1)} %get-tuple-element.50), channel_id=1, source_target_pairs={{12,8},{4,0},{13,9},{5,1},{14,10},{6,2},{15,11},{7,3},{28,24},{20,... | collective-permute-start | bytes 1572872 | tf_op jit(solution)/shard_map/ppermute | solution.py:401
  7.4 19.6 %collective-permute-start.1 = (bf16[512,512]{1,0:T(8,128)(2,1)}, bf16[512,512]{1,0:T(8,128)(2,1)S(1)}, u32[]{:S(2)}, u32[]{:S(2)}) collective-permute-start(bf16[512,512]{1,0:T(8,128)(2,1)} %get-tuple-element.51), channel_id=1, source_target_pairs={{8,4},{12,0},{9,5},{13,1},{10,6},{14,2},{11,7},{15,3},{24,20},{28,... | collective-permute-start | bytes 1572872 | tf_op jit(solution)/shard_map/ppermute | solution.py:401
  8.7 20.6 %collective-permute-start.2 = (bf16[512,512]{1,0:T(8,128)(2,1)}, bf16[512,512]{1,0:T(8,128)(2,1)S(1)}, u32[]{:S(2)}, u32[]{:S(2)}) collective-permute-start(bf16[512,512]{1,0:T(8,128)(2,1)} %get-tuple-element.52), channel_id=1, source_target_pairs={{8,12},{12,8},{9,13},{13,9},{10,14},{14,10},{11,15},{15,11},{24,28... | collective-permute-start | bytes 1572872 | tf_op jit(solution)/shard_map/ppermute | solution.py:401
  12.3 23.1 %collective-permute-start.3 = (bf16[2,512,512]{2,1,0:T(8,128)(2,1)}, bf16[2,512,512]{2,1,0:T(8,128)(2,1)}, u32[]{:S(2)}, u32[]{:S(2)}) collective-permute-start(bf16[2,512,512]{2,1,0:T(8,128)(2,1)} %get-tuple-element.61), channel_id=1, source_target_pairs={{0,4},{4,0},{1,5},{5,1},{2,6},{6,2},{3,7},{7,3},{16,20},{20,16},{1... | collective-permute-start | bytes 3145736 | tf_op jit(solution)/shard_map/ppermute | solution.py:401
  14.0 27.5 %collective-permute-start.4 = (bf16[2,512,512]{2,1,0:T(8,128)(2,1)}, bf16[2,512,512]{2,1,0:T(8,128)(2,1)}, u32[]{:S(2)}, u32[]{:S(2)}) collective-permute-start(bf16[2,512,512]{2,1,0:T(8,128)(2,1)} %get-tuple-element.62), channel_id=1, source_target_pairs={{0,12},{4,8},{1,13},{5,9},{2,14},{6,10},{3,15},{7,11},{16,28},{20,... | collective-permute-start | bytes 3145736 | tf_op jit(solution)/shard_map/ppermute | solution.py:401
  18.0 23.5 %copy-start = (bf16[128,8192]{1,0:T(8,128)(2,1)}, bf16[128,8192]{1,0:T(8,128)(2,1)S(1)}, u32[]{:S(2)}) copy-start(bf16[128,8192]{1,0:T(8,128)(2,1)S(1)} %multiply_convert_fusion.prod_ref) | copy-start | bytes 6291460
  27.0 5.1 %copy-start.1 = (bf16[512,512]{1,0:T(8,128)(2,1)}, bf16[512,512]{1,0:T(8,128)(2,1)S(1)}, u32[]{:S(2)}) copy-start(bf16[512,512]{1,0:T(8,128)(2,1)S(1)} %collective-permute-done.1.ql_ref) | copy-start | bytes 1572868
  29.3 2.8 %copy-start.2 = (bf16[512,512]{1,0:T(8,128)(2,1)}, bf16[512,512]{1,0:T(8,128)(2,1)S(1)}, u32[]{:S(2)}) copy-start(bf16[512,512]{1,0:T(8,128)(2,1)S(1)} %collective-permute-done.2.qr_ref) | copy-start | bytes 1572868
  42.6 8.7 %collective-permute-start.6 = (bf16[128,4096]{1,0:T(8,128)(2,1)S(1)}, bf16[128,4096]{1,0:T(8,128)(2,1)S(1)}, u32[]{:S(2)}, u32[]{:S(2)}) collective-permute-start(bf16[128,4096]{1,0:T(8,128)(2,1)S(1)} %get-tuple-element.73), channel_id=1, source_target_pairs={{3,7},{7,11},{11,15},{19,23},{23,27},{27,31},{35,39},{39,43},{43,4... | collective-permute-start | bytes 3145736 | tf_op jit(solution)/shard_map/ppermute | solution.py:447
  43.3 21.7 %collective-permute-start.5 = (bf16[128,4096]{1,0:T(8,128)(2,1)}, bf16[128,4096]{1,0:T(8,128)(2,1)}, u32[]{:S(2)}, u32[]{:S(2)}) collective-permute-start(bf16[128,4096]{1,0:T(8,128)(2,1)} %get-tuple-element.81), channel_id=1, source_target_pairs={{0,1},{1,2},{2,3},{3,4},{4,5},{5,6},{6,7},{7,8},{8,9},{9,10},{10,1... | collective-permute-start | bytes 3145736 | tf_op jit(solution)/shard_map/ppermute | solution.py:446
  51.5 19.5 %collective-permute-start.7 = (bf16[128,4096]{1,0:T(8,128)(2,1)S(1)}, bf16[128,4096]{1,0:T(8,128)(2,1)}, u32[]{:S(2)}, u32[]{:S(2)}) collective-permute-start(bf16[128,4096]{1,0:T(8,128)(2,1)S(1)} %broadcast_select_fusion), channel_id=1, source_target_pairs={{0,1},{1,2},{2,3},{3,0},{4,5},{5,6},{6,7},{7,4},{8,9},{9,10},{10,1... | collective-permute-start | bytes 3145736 | tf_op jit(solution)/shard_map/ppermute | solution.py:457
  57.8 23.4 %collective-permute-start.10 = (bf16[4,136,512]{2,1,0:T(8,128)(2,1)}, bf16[4,136,512]{2,1,0:T(8,128)(2,1)S(1)}, u32[]{:S(2)}, u32[]{:S(2)}) collective-permute-start(bf16[4,136,512]{2,1,0:T(8,128)(2,1)} %fold_early.1), channel_id=1, source_target_pairs={{0,4},{8,12},{1,5},{9,13},{2,6},{10,14},{3,7},{11,15},{16,20},{24,... | collective-permute-start | bytes 1671176 | tf_op jit(solution)/shard_map/ppermute | solution.py:401
  59.1 22.1 %collective-permute-start.8 = (bf16[4,136,512]{2,1,0:T(8,128)(2,1)}, bf16[4,136,512]{2,1,0:T(8,128)(2,1)S(1)}, u32[]{:S(2)}, u32[]{:S(2)}) collective-permute-start(bf16[4,136,512]{2,1,0:T(8,128)(2,1)} %get-tuple-element.69), channel_id=1, source_target_pairs={{0,12},{4,8},{1,13},{5,9},{2,14},{6,10},{3,15},{7,11},{16,28},{20,... | collective-permute-start | bytes 1671176 | tf_op jit(solution)/shard_map/ppermute | solution.py:401
  60.4 26.0 %collective-permute-start.9 = (bf16[4,136,512]{2,1,0:T(8,128)(2,1)}, bf16[4,136,512]{2,1,0:T(8,128)(2,1)S(1)}, u32[]{:S(2)}, u32[]{:S(2)}) collective-permute-start(bf16[4,136,512]{2,1,0:T(8,128)(2,1)} %get-tuple-element.69), channel_id=1, source_target_pairs={{8,12},{12,8},{9,13},{13,9},{10,14},{14,10},{11,15},{15,11},{24,28... | collective-permute-start | bytes 1671176 | tf_op jit(solution)/shard_map/ppermute | solution.py:401
  81.2 5.2 %copy-start.3 = (bf16[4,136,512]{2,1,0:T(8,128)(2,1)}, bf16[4,136,512]{2,1,0:T(8,128)(2,1)S(1)}, u32[]{:S(2)}) copy-start(bf16[4,136,512]{2,1,0:T(8,128)(2,1)S(1)} %collective-permute-done.10.three_ref) | copy-start | bytes 1671172
  81.2 5.2 %copy-start.4 = (bf16[4,136,512]{2,1,0:T(8,128)(2,1)}, bf16[4,136,512]{2,1,0:T(8,128)(2,1)S(1)}, u32[]{:S(2)}) copy-start(bf16[4,136,512]{2,1,0:T(8,128)(2,1)S(1)} %collective-permute-done.8.one_ref) | copy-start | bytes 1671172
  86.4 0.8 copy-start.5

commit v4 on v3

--- a/solution.py
+++ b/solution.py
@@ -14,7 +14,7 @@
 SIDE = 4
 SUB = 256
 EXTRA = 8
-COLS = 2048
+COLS = 4096
 HEADS_AXIS = 4
 
 

time: 91.8 us -> 91.8 us (level); the launches traced: 91.2 us -> 90.2 us
  starting transfers between devices: 27.6 us -> 23.3 us
  Pallas kernels: 37.7 us -> 41.4 us
    ppermute x1, starting transfers between devices: 6.35 us -> 2.09 us  [on_device(): lax.ppermute(jnp.where(at_head == heads - 1, staged, prod_b), 'head', [(i...]
    pallas_call x4, Pallas kernels: 20.3 us -> 23.6 us  [fold_call(): pl.pallas_call(kernel, out_shape=out_shape, grid_spec=pltpu.PrefetchScala...]
    ppermute x8, waiting for transfers between devices: 13.5 us -> 11.9 us  [pass_on(): return lax.ppermute(x, 'ctx', list(pairs))]
    ppermute x1, waiting for transfers between devices: 5.99 us -> 7.02 us  [on_device(): lax.ppermute(jnp.where(at_head == heads - 1, staged, prod_b), 'head', [(i...]
  transfers between devices with their start and end apart: 11 -> 11, of which waited for: 4 -> 4; matrix products, arithmetic and copies ran while one was open for 4% -> 4% of each run, Pallas kernels for 33% -> 38%
where the time goes in v4:
time: 91.8 us; the launch traced here: 90.2 us
  Pallas kernels  41.4 us (45%)
  starting transfers between devices  23.3 us (25%)
  waiting for transfers between devices  19 us (21%)
  other arithmetic  3.68 us (4%)
  local copies, waits for them, and re-layouts  1.99 us (2%)
    pallas_call x4, Pallas kernels, fold_call(): pl.pallas_call(kernel, out_shape=out_shape, grid_spec=pltpu.PrefetchScala...  23.6 us
    ppermute x8, starting transfers between devices, pass_on(): return lax.ppermute(x, 'ctx', list(pairs))  18.6 us
    ppermute x8, waiting for transfers between devices, pass_on(): return lax.ppermute(x, 'ctx', list(pairs))  11.9 us
    pallas_call x1, Pallas kernels, mixer(): pl.pallas_call(functools.partial(conv_kernel, group_size), out_shape=jax....  10.7 us
    ppermute x1, waiting for transfers between devices, on_device(): lax.ppermute(jnp.where(at_head == heads - 1, staged, prod_b), 'head', [(i...  7.02 us
    pallas_call x1, Pallas kernels, merge(): pl.pallas_call(merge_kernel, out_shape=jax.ShapeDtypeStruct((rows, 2 * SI...  4 us
    pallas_call x1, Pallas kernels, pack(): pl.pallas_call(pack_kernel, out_shape=(both, both, single, single, single...  3.15 us
    convert_element_type x1, other arithmetic, on_device(): (mix_key.astype(jnp.float32) * mix_value.astype(jnp.float32)).astype(jnp....  2.71 us
  transfers between devices with their start and end apart: 11, of which 4 were waited for; matrix products, arithmetic and copies ran while one was open for 4% of the time, Pallas kernels for 38%

profile of v4, /device:TPU:118, one launch (start us, length us, event | category | flops | bytes accessed | tf_op | source)
XLA Modules:
  0.0 90.2 jit_solution(14374027203436639194)
XLA Ops:
  0.6 3.1 %pack.1 = (bf16[2,512,512]{2,1,0:T(8,128)(2,1)}, bf16[2,512,512]{2,1,0:T(8,128)(2,1)}, bf16[512,512]{1,0:T(8,128)(2,1)}, bf16[512,512]{1,0:T(8,128)(2,1)}, bf16[512,512]{1,0:T(8,128)(2,1)}) custom-call(s32[1]{0:T(128)} %bitcast.place, bf16[512,1024]{1,0:T(8,128)(2,1)} %q_ref.3, bf16[512,1024]{1,0:T(8,128)(2,1)} %k_ref.7, bf16[512,1024]{1,0:T(8,128)(2,1)} %v_ref.7), custom_call_target="tpu_custom_call" | custom-call | tf_op jit(solution)/shard_map/pack/pallas_call | solution.py:323
  3.8 0.0 copy-start.6
  3.8 3.6 %collective-permute-start = (bf16[512,512]{1,0:T(8,128)(2,1)}, bf16[512,512]{1,0:T(8,128)(2,1)}, u32[]{:S(2)}, u32[]{:S(2)}) collective-permute-start(bf16[512,512]{1,0:T(8,128)(2,1)} %get-tuple-element.50), channel_id=1, source_target_pairs={{12,8},{4,0},{13,9},{5,1},{14,10},{6,2},{15,11},{7,3},{28,24},{20,... | collective-permute-start | bytes 1572872 | tf_op jit(solution)/shard_map/ppermute | solution.py:401
  7.4 1.3 %collective-permute-start.1 = (bf16[512,512]{1,0:T(8,128)(2,1)}, bf16[512,512]{1,0:T(8,128)(2,1)S(1)}, u32[]{:S(2)}, u32[]{:S(2)}) collective-permute-start(bf16[512,512]{1,0:T(8,128)(2,1)} %get-tuple-element.51), channel_id=1, source_target_pairs={{8,4},{12,0},{9,5},{13,1},{10,6},{14,2},{11,7},{15,3},{24,20},{28,... | collective-permute-start | bytes 1572872 | tf_op jit(solution)/shard_map/ppermute | solution.py:401
  8.7 3.6 %collective-permute-start.2 = (bf16[512,512]{1,0:T(8,128)(2,1)}, bf16[512,512]{1,0:T(8,128)(2,1)S(1)}, u32[]{:S(2)}, u32[]{:S(2)}) collective-permute-start(bf16[512,512]{1,0:T(8,128)(2,1)} %get-tuple-element.52), channel_id=1, source_target_pairs={{8,12},{12,8},{9,13},{13,9},{10,14},{14,10},{11,15},{15,11},{24,28... | collective-permute-start | bytes 1572872 | tf_op jit(solution)/shard_map/ppermute | solution.py:401
  12.3 1.7 %collective-permute-start.3 = (bf16[2,512,512]{2,1,0:T(8,128)(2,1)}, bf16[2,512,512]{2,1,0:T(8,128)(2,1)}, u32[]{:S(2)}, u32[]{:S(2)}) collective-permute-start(bf16[2,512,512]{2,1,0:T(8,128)(2,1)} %get-tuple-element.61), channel_id=1, source_target_pairs={{0,4},{4,0},{1,5},{5,1},{2,6},{6,2},{3,7},{7,3},{16,20},{20,16},{1... | collective-permute-start | bytes 3145736 | tf_op jit(solution)/shard_map/ppermute | solution.py:401
  14.0 1.3 %collective-permute-start.4 = (bf16[2,512,512]{2,1,0:T(8,128)(2,1)}, bf16[2,512,512]{2,1,0:T(8,128)(2,1)}, u32[]{:S(2)}, u32[]{:S(2)}) collective-permute-start(bf16[2,512,512]{2,1,0:T(8,128)(2,1)} %get-tuple-element.62), channel_id=1, source_target_pairs={{0,12},{4,8},{1,13},{5,9},{2,14},{6,10},{3,15},{7,11},{16,28},{20,... | collective-permute-start | bytes 3145736 | tf_op jit(solution)/shard_map/ppermute | solution.py:401
  15.3 2.7 %multiply_convert_fusion.prod_ref = bf16[128,8192]{1,0:T(8,128)(2,1)S(1)} fusion(bf16[128,8192]{1,0:T(8,128)(2,1)} %param.10, bf16[128,8192]{1,0:T(8,128)(2,1)} %param.9), kind=kLoop, calls=%fused_computation | loop fusion | flops 4194304 | bytes 6291456 | tf_op jit(solution)/shard_map/convert_element_type | solution.py:415
  18.0 0.0 copy-done.6
  18.0 0.0 copy-start
  18.0 0.8 convert_reduce_fusion.bounds
  18.9 8.2 %fold_own.1 = (f32[8,128,512]{2,1,0:T(8,128)}, f32[8,8,512]{2,1,0:T(8,128)}) custom-call(s32[1]{0:T(128)} %bitcast.place, s32[4]{0:T(128)} %convert_reduce_fusion.bounds, bf16[512,1024]{1,0:T(8,128)(2,1)} %q_ref.3, bf16[512,1024]{1,0:T(8,128)(2,1)} %k_ref.7, bf16[512,1024]{1,0:T(8,128)(2,1)} %v_ref.7), custom_call_target="tpu_custom_call" | custom-call | flops 1 | bytes 1 | tf_op jit(solution)/shard_map/fold_own/pallas_call | solution.py:280
  27.0 0.0 collective-permute-done.q_ref
  27.0 0.0 collective-permute-done.1.ql_ref
  27.0 0.0 copy-start.1
  27.0 2.2 %collective-permute-done.2.qr_ref = bf16[512,512]{1,0:T(8,128)(2,1)S(1)} collective-permute-done((bf16[512,512]{1,0:T(8,128)(2,1)}, bf16[512,512]{1,0:T(8,128)(2,1)S(1)}, u32[]{:S(2)}, u32[]{:S(2)}) %collective-permute-start.2) | collective-permute-done | bytes 524320 | tf_op jit(solution)/shard_map/ppermute | solution.py:401
  29.3 0.0 copy-start.2
  29.3 2.8 %fold_early.1 = bf16[4,136,512]{2,1,0:T(8,128)(2,1)} custom-call(s32[1]{0:T(128)} %bitcast.place, s32[4]{0:T(128)} %convert_reduce_fusion.bounds, bf16[512,512]{1,0:T(8,128)(2,1)} %collective-permute-done.q_ref, bf16[512,1024]{1,0:T(8,128)(2,1)} %k_ref.7, bf16[512,1024]{1,0:T(8,128)(2,1)} %v_ref.7), custom_call_target="tpu_custom_call" | custom-call | flops 1 | bytes 1 | tf_op jit(solution)/shard_map/fold_early/pallas_call | solution.py:280
  32.1 0.0 copy-done.1
  32.1 0.0 copy-done.2
  32.1 3.3 %fold_carry.1 = (f32[4,128,512]{2,1,0:T(8,128)}, f32[4,8,512]{2,1,0:T(8,128)}) custom-call(s32[1]{0:T(128)} %bitcast.place, s32[4]{0:T(128)} %convert_reduce_fusion.bounds, bf16[512,512]{1,0:T(8,128)(2,1)} %copy-done.1, bf16[512,512]{1,0:T(8,128)(2,1)} %copy-done.2, bf16[512,1024]{1,0:T(8,128)(2,1)} %k_ref.7, bf16[512,1024]{1,0:T(8,128)(2,1)} %v_ref.7), custom_call_target="tpu_custom_call" | custom-call | flops 1 | bytes 1 | tf_op jit(solution)/shard_map/fold_carry/pallas_call | solution.py:280
  35.4 0.0 collective-permute-done.3.left_ref
  35.4 6.1 %collective-permute-done.4.right_ref = bf16[2,512,512]{2,1,0:T(8,128)(2,1)} collective-permute-done((bf16[2,512,512]{2,1,0:T(8,128)(2,1)}, bf16[2,512,512]{2,1,0:T(8,128)(2,1)}, u32[]{:S(2)}, u32[]{:S(2)}) %collective-permute-start.4) | collective-permute-done | bytes 1048608 | tf_op jit(solution)/shard_map/ppermute | solution.py:401
  41.4 0.0 copy-done
  41.4 1.2 %fusion = (bf16[128,4096]{1,0:T(8,128)(2,1)S(1)}, bf16[128,4096]{1,0:T(8,128)(2,1)}) fusion(bf16[128,8192]{1,0:T(8,128)(2,1)S(1)} %multiply_convert_fusion.prod_ref), kind=kLoop, calls=%fused_computation.4 | loop fusion | bytes 4194304 | tf_op jit(solution)/shard_map/slice | solution.py:445
  42.6 0.7 collective-permute-start.6
  43.3 1.9 %collective-permute-start.5 = (bf16[128,4096]{1,0:T(8,128)(2,1)}, bf16[128,4096]{1,0:T(8,128)(2,1)}, u32[]{:S(2)}, u32[]{:S(2)}) collective-permute-start(bf16[128,4096]{1,0:T(8,128)(2,1)} %get-tuple-element.81), channel_id=1, source_target_pairs={{0,1},{1,2},{2,3},{3,4},{4,5},{5,6},{6,7},{7,8},{8,9},{9,10},{10,1... | collective-permute-start | bytes 3145736 | tf_op jit(solution)/shard_map/ppermute | solution.py:446
  45.3 9.3 %fold_late.1 = (bf16[4,136,512]{2,1,0:T(8,128)(2,1)}, f32[4,128,512]{2,1,0:T(8,128)}, f32[4,8,512]{2,1,0:T(8,128)}) custom-call(s32[1]{0:T(128)} %bitcast.place, s32[4]{0:T(128)} %convert_reduce_fusion.bounds, bf16[512,512]{1,0:T(8,128)(2,1)} %copy-done.1, bf16[512,512]{1,0:T(8,128)(2,1)} %copy-done.2, f32[4,128,512]{2,1,0:T(8,128)} %get-tuple-element.65.part_ref, ...), custom_call_target="tpu_custom_call" | custom-call | flops 1 | bytes 1 | tf_op jit(solution)/shard_map/fold_late/pallas_call | solution.py:280
  54.6 0.0 collective-permute-done.6
  54.6 0.1 broadcast_select_fusion
  54.7 2.1 %collective-permute-start.7 = (bf16[128,4096]{1,0:T(8,128)(2,1)S(1)}, bf16[128,4096]{1,0:T(8,128)(2,1)}, u32[]{:S(2)}, u32[]{:S(2)}) collective-permute-start(bf16[128,4096]{1,0:T(8,128)(2,1)S(1)} %broadcast_select_fusion), channel_id=1, source_target_pairs={{0,1},{1,2},{2,3},{3,0},{4,5},{5,6},{6,7},{7,4},{8,9},{9,10},{10,1... | collective-permute-start | bytes 3145736 | tf_op jit(solution)/shard_map/ppermute | solution.py:457
  56.8 1.3 %collective-permute-start.10 = (bf16[4,136,512]{2,1,0:T(8,128)(2,1)}, bf16[4,136,512]{2,1,0:T(8,128)(2,1)S(1)}, u32[]{:S(2)}, u32[]{:S(2)}) collective-permute-start(bf16[4,136,512]{2,1,0:T(8,128)(2,1)} %fold_early.1), channel_id=1, source_target_pairs={{0,4},{8,12},{1,5},{9,13},{2,6},{10,14},{3,7},{11,15},{16,20},{24,... | collective-permute-start | bytes 1671176 | tf_op jit(solution)/shard_map/ppermute | solution.py:401
  58.1 1.3 %collective-permute-start.8 = (bf16[4,136,512]{2,1,0:T(8,128)(2,1)}, bf16[4,136,512]{2,1,0:T(8,128)(2,1)S(1)}, u32[]{:S(2)}, u32[]{:S(2)}) collective-permute-start(bf16[4,136,512]{2,1,0:T(8,128)(2,1)} %get-tuple-element.69), channel_id=1, source_target_pairs={{0,12},{4,8},{1,13},{5,9},{2,14},{6,10},{3,15},{7,11},{16,28},{20,... | collective-permute-start | bytes 1671176 | tf_op jit(solution)/shard_map/ppermute | solution.py:401
  59.4 4.6 %collective-permute-start.9 = (bf16[4,136,512]{2,1,0:T(8,128)(2,1)}, bf16[4,136,512]{2,1,0:T(8,128)(2,1)S(1)}, u32[]{:S(2)}, u32[]{:S(2)}) collective-permute-start(bf16[4,136,512]{2,1,0:T(8,128)(2,1)} %get-tuple-element.69), channel_id=1, source_target_pairs={{8,12},{12,8},{9,13},{13,9},{10,14},{14,10},{11,15},{15,11},{24,28... | collective-permute-start | bytes 1671176 | tf_op jit(solution)/shard_map/ppermute | solution.py:401
  64.0 0.0 collective-permute-done.5.rim_a_ref
  64.0 7.0 %collective-permute-done.7.rim_b_ref = bf16[128,4096]{1,0:T(8,128)(2,1)} collective-permute-done((bf16[128,4096]{1,0:T(8,128)(2,1)S(1)}, bf16[128,4096]{1,0:T(8,128)(2,1)}, u32[]{:S(2)}, u32[]{:S(2)}) %collective-permute-start.7) | collective-permute-done | bytes 1048608 | tf_op jit(solution)/shard_map/ppermute | solution.py:457
  71.0 10.7 %mixer.1 = bf16[128,8192]{1,0:T(8,128)(2,1)} custom-call(s32[1]{0:T(128)} %bitcast.place, s32[4]{0:T(128)} %convert_reduce_fusion.bounds, bf16[128,4096]{1,0:T(8,128)(2,1)} %collective-permute-done.5.rim_a_ref, bf16[128,4096]{1,0:T(8,128)(2,1)} %collective-permute-done.7.rim_b_ref, bf16[128,8192]{1,0:T(8,128)(2,1)} %copy-done, bf16[128,8192]{1,0:T(8,128)(2,1)} %query_ref.1, ...), custom_call_target="tpu_custom_call" | custom-call | flops 8589934592 | bytes 8388608 | tf_op jit(solution)/shard_map/mixer/pallas_call | solution.py:68
  81.7 0.0 collective-permute-done.10.three_ref
  81.7 0.0 copy-start.3
  81.7 0.0 collective-permute-done.8.one_ref
  81.7 0.0 copy-start.4
  81.7 3.6 %collective-permute-done.9.two_ref = bf16[4,136,512]{2,1,0:T(8,128)(2,1)S(1)} collective-permute-done((bf16[4,136,512]{2,1,0:T(8,128)(2,1)}, bf16[4,136,512]{2,1,0:T(8,128)(2,1)S(1)}, u32[]{:S(2)}, u32[]{:S(2)}) %collective-permute-start.9) | collective-permute-done | bytes 557088 | tf_op jit(solution)/shard_map/ppermute | solution.py:401
  85.4 0.0 copy-done.3
  85.4 0.0 copy-done.4
  85.4 0.0 copy-start.5
  85.4 0.8 copy-done.5
  86.2 4.0 %merge.1 = bf16[512,1024]{1,0:T(8,128)(2,1)} custom-call(s32[1]{0:T(128)} %bitcast.place, f32[8,128,512]{2,1,0:T(8,128)} %get-tuple-element.76.own, f32[8,8,512]{2,1,0:T(8,128)} %get-tuple-element.77.own_lse, f32[4,128,512]{2,1,0:T(8,128)} %get-tuple-element.78.got, f32[4,8,512]{2,1,0:T(8,128)} %get-tuple-element.79.got_lse, bf16[4,136,512]{2,1,0:T(8,128)(2,1)} %copy-done.4, ...), custom_call_target="tpu_custom_call" | custom-call | tf_op jit(solution)/shard_map/merge/pallas_call | solution.py:380
Async XLA Ops:
  3.8 14.2 %copy-start.6 = (s32[2048]{0:T(1024)S(1)}, s32[2048]{0:T(1024)}, u32[]{:S(2)}) copy-start(s32[2048]{0:T(1024)} %param.12) | copy-start | bytes 24580
  3.8 23.2 %collective-permute-start = (bf16[512,512]{1,0:T(8,128)(2,1)}, bf16[512,512]{1,0:T(8,128)(2,1)}, u32[]{:S(2)}, u32[]{:S(2)}) collective-permute-start(bf16[512,512]{1,0:T(8,128)(2,1)} %get-tuple-element.50), channel_id=1, source_target_pairs={{12,8},{4,0},{13,9},{5,1},{14,10},{6,2},{15,11},{7,3},{28,24},{20,... | collective-permute-start | bytes 1572872 | tf_op jit(solution)/shard_map/ppermute | solution.py:401
  7.4 19.6 %collective-permute-start.1 = (bf16[512,512]{1,0:T(8,128)(2,1)}, bf16[512,512]{1,0:T(8,128)(2,1)S(1)}, u32[]{:S(2)}, u32[]{:S(2)}) collective-permute-start(bf16[512,512]{1,0:T(8,128)(2,1)} %get-tuple-element.51), channel_id=1, source_target_pairs={{8,4},{12,0},{9,5},{13,1},{10,6},{14,2},{11,7},{15,3},{24,20},{28,... | collective-permute-start | bytes 1572872 | tf_op jit(solution)/shard_map/ppermute | solution.py:401
  8.7 20.6 %collective-permute-start.2 = (bf16[512,512]{1,0:T(8,128)(2,1)}, bf16[512,512]{1,0:T(8,128)(2,1)S(1)}, u32[]{:S(2)}, u32[]{:S(2)}) collective-permute-start(bf16[512,512]{1,0:T(8,128)(2,1)} %get-tuple-element.52), channel_id=1, source_target_pairs={{8,12},{12,8},{9,13},{13,9},{10,14},{14,10},{11,15},{15,11},{24,28... | collective-permute-start | bytes 1572872 | tf_op jit(solution)/shard_map/ppermute | solution.py:401
  12.3 23.1 %collective-permute-start.3 = (bf16[2,512,512]{2,1,0:T(8,128)(2,1)}, bf16[2,512,512]{2,1,0:T(8,128)(2,1)}, u32[]{:S(2)}, u32[]{:S(2)}) collective-permute-start(bf16[2,512,512]{2,1,0:T(8,128)(2,1)} %get-tuple-element.61), channel_id=1, source_target_pairs={{0,4},{4,0},{1,5},{5,1},{2,6},{6,2},{3,7},{7,3},{16,20},{20,16},{1... | collective-permute-start | bytes 3145736 | tf_op jit(solution)/shard_map/ppermute | solution.py:401
  14.0 27.5 %collective-permute-start.4 = (bf16[2,512,512]{2,1,0:T(8,128)(2,1)}, bf16[2,512,512]{2,1,0:T(8,128)(2,1)}, u32[]{:S(2)}, u32[]{:S(2)}) collective-permute-start(bf16[2,512,512]{2,1,0:T(8,128)(2,1)} %get-tuple-element.62), channel_id=1, source_target_pairs={{0,12},{4,8},{1,13},{5,9},{2,14},{6,10},{3,15},{7,11},{16,28},{20,... | collective-permute-start | bytes 3145736 | tf_op jit(solution)/shard_map/ppermute | solution.py:401
  18.0 23.5 %copy-start = (bf16[128,8192]{1,0:T(8,128)(2,1)}, bf16[128,8192]{1,0:T(8,128)(2,1)S(1)}, u32[]{:S(2)}) copy-start(bf16[128,8192]{1,0:T(8,128)(2,1)S(1)} %multiply_convert_fusion.prod_ref) | copy-start | bytes 6291460
  27.0 5.1 %copy-start.1 = (bf16[512,512]{1,0:T(8,128)(2,1)}, bf16[512,512]{1,0:T(8,128)(2,1)S(1)}, u32[]{:S(2)}) copy-start(bf16[512,512]{1,0:T(8,128)(2,1)S(1)} %collective-permute-done.1.ql_ref) | copy-start | bytes 1572868
  29.3 2.8 %copy-start.2 = (bf16[512,512]{1,0:T(8,128)(2,1)}, bf16[512,512]{1,0:T(8,128)(2,1)S(1)}, u32[]{:S(2)}) copy-start(bf16[512,512]{1,0:T(8,128)(2,1)S(1)} %collective-permute-done.2.qr_ref) | copy-start | bytes 1572868
  42.6 12.0 %collective-permute-start.6 = (bf16[128,4096]{1,0:T(8,128)(2,1)S(1)}, bf16[128,4096]{1,0:T(8,128)(2,1)S(1)}, u32[]{:S(2)}, u32[]{:S(2)}) collective-permute-start(bf16[128,4096]{1,0:T(8,128)(2,1)S(1)} %get-tuple-element.73), channel_id=1, source_target_pairs={{3,7},{7,11},{11,15},{19,23},{23,27},{27,31},{35,39},{39,43},{43,4... | collective-permute-start | bytes 3145736 | tf_op jit(solution)/shard_map/ppermute | solution.py:447
  43.3 20.6 %collective-permute-start.5 = (bf16[128,4096]{1,0:T(8,128)(2,1)}, bf16[128,4096]{1,0:T(8,128)(2,1)}, u32[]{:S(2)}, u32[]{:S(2)}) collective-permute-start(bf16[128,4096]{1,0:T(8,128)(2,1)} %get-tuple-element.81), channel_id=1, source_target_pairs={{0,1},{1,2},{2,3},{3,4},{4,5},{5,6},{6,7},{7,8},{8,9},{9,10},{10,1... | collective-permute-start | bytes 3145736 | tf_op jit(solution)/shard_map/ppermute | solution.py:446
  54.7 16.3 %collective-permute-start.7 = (bf16[128,4096]{1,0:T(8,128)(2,1)S(1)}, bf16[128,4096]{1,0:T(8,128)(2,1)}, u32[]{:S(2)}, u32[]{:S(2)}) collective-permute-start(bf16[128,4096]{1,0:T(8,128)(2,1)S(1)} %broadcast_select_fusion), channel_id=1, source_target_pairs={{0,1},{1,2},{2,3},{3,0},{4,5},{5,6},{6,7},{7,4},{8,9},{9,10},{10,1... | collective-permute-start | bytes 3145736 | tf_op jit(solution)/shard_map/ppermute | solution.py:457
  56.8 24.9 %collective-permute-start.10 = (bf16[4,136,512]{2,1,0:T(8,128)(2,1)}, bf16[4,136,512]{2,1,0:T(8,128)(2,1)S(1)}, u32[]{:S(2)}, u32[]{:S(2)}) collective-permute-start(bf16[4,136,512]{2,1,0:T(8,128)(2,1)} %fold_early.1), channel_id=1, source_target_pairs={{0,4},{8,12},{1,5},{9,13},{2,6},{10,14},{3,7},{11,15},{16,20},{24,... | collective-permute-start | bytes 1671176 | tf_op jit(solution)/shard_map/ppermute | solution.py:401
  58.1 23.6 %collective-permute-start.8 = (bf16[4,136,512]{2,1,0:T(8,128)(2,1)}, bf16[4,136,512]{2,1,0:T(8,128)(2,1)S(1)}, u32[]{:S(2)}, u32[]{:S(2)}) collective-permute-start(bf16[4,136,512]{2,1,0:T(8,128)(2,1)} %get-tuple-element.69), channel_id=1, source_target_pairs={{0,12},{4,8},{1,13},{5,9},{2,14},{6,10},{3,15},{7,11},{16,28},{20,... | collective-permute-start | bytes 1671176 | tf_op jit(solution)/shard_map/ppermute | solution.py:401
  59.4 26.0 %collective-permute-start.9 = (bf16[4,136,512]{2,1,0:T(8,128)(2,1)}, bf16[4,136,512]{2,1,0:T(8,128)(2,1)S(1)}, u32[]{:S(2)}, u32[]{:S(2)}) collective-permute-start(bf16[4,136,512]{2,1,0:T(8,128)(2,1)} %get-tuple-element.69), channel_id=1, source_target_pairs={{8,12},{12,8},{9,13},{13,9},{10,14},{14,10},{11,15},{15,11},{24,28... | collective-permute-start | bytes 1671176 | tf_op jit(solution)/shard_map/ppermute | solution.py:401
  81.7 3.7 %copy-start.3 = (bf16[4,136,512]{2,1,0:T(8,128)(2,1)}, bf16[4,136,512]{2,1,0:T(8,128)(2,1)S(1)}, u32[]{:S(2)}) copy-start(bf16[4,136,512]{2,1,0:T(8,128)(2,1)S(1)} %collective-permute-done.10.three_ref) | copy-start | bytes 1671172
  81.7 3.7 %copy-start.4 = (bf16[4,136,512]{2,1,0:T(8,128)(2,1)}, bf16[4,136,512]{2,1,0:T(8,128)(2,1)S(1)}, u32[]{:S(2)}) copy-start(bf16[4,136,512]{2,1,0:T(8,128)(2,1)S(1)} %collective-permute-done.8.one_ref) | copy-start | bytes 1671172
  85.4 0.8 copy-start.5
